TPU v7x, 1024 devices: a whole 4x8x16 slice. The times are simulated.
1024 devices in a mesh: row: 16 (over z_lo, core), col: 64 (over y, z_hi, x).
Axes of the slice: x: 4, y: 8, z: 16 (z_hi: 2, z_lo: 8; z = z_hi * 8 + z_lo), core: 2. Of those that a mesh axis runs over, the one named last changes fastest.
Arguments:
- vectors: float32 [8192, 16384], P('row', 'col'), may hold values from -6 to 6
- reflectors: float32 [4, 8192, 256], P(None, ('row', 'col')), may hold values from -6 to 6
- owner_list: int32 [128], replicated, may hold values from 0 to 63, as said below
- slot_list: int32 [128], replicated, may hold values from 0 to 1
Outputs:
- result: float32 [8192, 16384], P('row', 'col')
Inputs may be any that keep to these rules, and one draw needn't show every extreme that they name: owner_list * 2 + slot_list takes each value 0 to 127 exactly once.
All inputs are finite; a program needn't handle non-finite values.
Results may differ from a plain program's by a relative error of at most 0.0001.
Values sent between devices are 32-bit elements; how exact they have to be, the bound alone decides.
A program may use at most 64 MiB of HBM per device.

v0:
```python
import jax
import jax.numpy as jnp
from jax import lax
from jax.sharding import PartitionSpec as P

BW = 128
BLK_DEV = 2
PANELS = 4


def matmul(left, right):
    return jnp.dot(left, right, precision=lax.Precision.HIGHEST, preferred_element_type=jnp.float32)


def upper_inverse(upper):
    order = upper.shape[0]
    if order <= 16:
        diag_vals = jnp.diagonal(upper)
        nilpotent = -(jnp.triu(upper, 1) / diag_vals[:, None])
        accum = jnp.eye(order, dtype=jnp.float32) + nilpotent
        power = nilpotent
        for _ in range(max((order - 1).bit_length() - 1, 0)):
            power = matmul(power, power)
            accum = accum + matmul(accum, power)
        return accum * (1.0 / diag_vals)[None, :]
    half = order // 2
    first_inv = upper_inverse(upper[:half, :half])
    second_inv = upper_inverse(upper[half:, half:])
    corner = -matmul(matmul(first_inv, upper[:half, half:]), second_inv)
    top_part = jnp.concatenate([first_inv, corner], axis=1)
    low_part = jnp.concatenate([jnp.zeros((order - half, half), jnp.float32), second_inv], axis=1)
    return jnp.concatenate([top_part, low_part], axis=0)


def resort(slab_now, owner_list, slot_list):
    spread = lax.all_to_all(slab_now, "col", split_axis=0, concat_axis=1, tiled=True)
    blocks = owner_list.shape[0]
    target = owner_list * BLK_DEV + slot_list
    positions = jnp.arange(blocks, dtype=jnp.int32)
    one_hot = (target[:, None] == positions[None, :]).astype(jnp.float32)
    blocks_view = spread.reshape(spread.shape[0], blocks, BW)
    ordered = jnp.einsum(
        "rbw,bc->rcw",
        blocks_view,
        one_hot,
        precision=lax.Precision.HIGHEST,
        preferred_element_type=jnp.float32,
    )
    ordered = ordered.reshape(spread.shape[0], blocks * BW)
    return lax.all_to_all(ordered, "col", split_axis=1, concat_axis=0, tiled=True)


def update_slab(slab_now, panel_rows, gram_sum, product):
    upper_form = jnp.triu(gram_sum, 1) + jnp.diag(jnp.diagonal(gram_sum) * 0.5)
    coefficients = matmul(upper_inverse(upper_form), product)
    return slab_now - matmul(panel_rows, coefficients)


def on_device(vectors, reflectors, owner_list, slot_list):
    gathered = lax.all_gather(reflectors, "col", axis=1, tiled=True)
    slab_now = vectors
    slab_now = resort(slab_now, owner_list, slot_list)
    for panel_index in reversed(range(PANELS)):
        panel_rows = gathered[panel_index]
        local_product = matmul(panel_rows.T, slab_now)
        local_gram = matmul(panel_rows.T, panel_rows)
        gram_sum, product = lax.psum((local_gram, local_product), "row")
        slab_now = update_slab(slab_now, panel_rows, gram_sum, product)
    return slab_now


def solution(mesh):
    return jax.shard_map(
        on_device,
        mesh=mesh,
        in_specs=(P("row", "col"), P(None, ("row", "col"), None), P(), P()),
        out_specs=P("row", "col"),
        check_vma=False,
    )
```

profile of v0, /device:TPU:1, one launch (start us, length us, event | category | flops | bytes accessed | tf_op | source)
XLA Modules:
  0.0 1297.8 jit_solution(12685867063928412848)
XLA Ops:
  6.5 28.0 %all-to-all-start = ((f32[64,8,256]{2,1,0:T(8,128)}), f32[64,8,256]{2,1,0:T(8,128)S(1)}, u32[]{:S(2)}, u32[]{:S(2)}) async-start(f32[64,8,256]{2,1,0:T(8,128)} %bitcast.805), calls=%async_computation | async-start | bytes 1048576 | tf_op jit(solution)/shard_map/all_to_all | solution.py:36
  36.0 20.5 %all-to-all-done = f32[64,8,256]{2,1,0:T(8,128)S(1)} async-done(((f32[64,8,256]{2,1,0:T(8,128)}), f32[64,8,256]{2,1,0:T(8,128)S(1)}, u32[]{:S(2)}, u32[]{:S(2)}) %all-to-all-start) | async-done | bytes 524320 | tf_op jit(solution)/shard_map/all_to_all | solution.py:36
  57.2 1.1 copy.13
  58.3 10.1 all-to-all-start.1
  68.5 152.7 %all-gather.2.cloned.1.call-done = f32[4,512,256]{2,1,0:T(8,128)} async-done(((f32[4,8,256]{2,1,0:T(8,128)}), f32[4,512,256]{2,1,0:T(8,128)}) %all-gather.2.cloned.1.call-update) | async-done | bytes 2097168 | tf_op jit(solution)/shard_map/all_gather | solution.py:60
  221.2 3.1 fusion.68
  224.3 2.8 convolution_bitcast_fusion.8
  227.9 1.7 fusion.69
  229.6 194.4 %all-reduce.75.cloned.1.call-done = (f32[256,256]{0,1:T(8,128)}, f32[256,256]{1,0:T(8,128)}) async-done(((f32[256,256]{0,1:T(8,128)}, f32[256,256]{1,0:T(8,128)}), (f32[256,256]{0,1:T(8,128)}, f32[256,256]{1,0:T(8,128)})) %all-reduce.75.cloned.1.call-update) | async-done | bytes 524304 | tf_op jit(solution)/shard_map/psum | solution.py:67
  424.0 2.6 gather_fusion
  484.8 1.1 fusion
  485.9 1.3 convolution_bitcast_fusion.7
  487.4 1.7 fusion.70
  489.2 202.7 %all-reduce.73.cloned.1.call-done = (f32[256,256]{0,1:T(8,128)}, f32[256,256]{1,0:T(8,128)}) async-done(((f32[256,256]{0,1:T(8,128)}, f32[256,256]{1,0:T(8,128)}), (f32[256,256]{0,1:T(8,128)}, f32[256,256]{1,0:T(8,128)})) %all-reduce.73.cloned.1.call-update) | async-done | bytes 524304 | tf_op jit(solution)/shard_map/psum | solution.py:67
  691.9 2.6 gather_fusion.17
  752.7 1.1 fusion.1
  753.8 1.3 convolution_bitcast_fusion.6
  755.4 1.7 fusion.71
  757.1 202.8 %all-reduce.71.cloned.1.call-done = (f32[256,256]{0,1:T(8,128)}, f32[256,256]{1,0:T(8,128)}) async-done(((f32[256,256]{0,1:T(8,128)}, f32[256,256]{1,0:T(8,128)}), (f32[256,256]{0,1:T(8,128)}, f32[256,256]{1,0:T(8,128)})) %all-reduce.71.cloned.1.call-update) | async-done | bytes 524304 | tf_op jit(solution)/shard_map/psum | solution.py:67
  959.9 2.6 gather_fusion.34
  1021.8 1.3 convolution_bitcast_fusion.5
  1023.1 204.8 %all-reduce.69.cloned.1.call-done = (f32[256,256]{0,1:T(8,128)}, f32[256,256]{1,0:T(8,128)}) async-done(((f32[256,256]{0,1:T(8,128)}, f32[256,256]{1,0:T(8,128)}), (f32[256,256]{0,1:T(8,128)}, f32[256,256]{1,0:T(8,128)})) %all-reduce.69.cloned.1.call-update) | async-done | bytes 524304 | tf_op jit(solution)/shard_map/psum | solution.py:67
  1227.9 2.6 gather_fusion.51
  1289.0 1.1 fusion.3
  (751 shorter events, 237.8 us)
Async XLA Ops:
  6.5 49.9 %all-to-all-start = ((f32[64,8,256]{2,1,0:T(8,128)}), f32[64,8,256]{2,1,0:T(8,128)S(1)}, u32[]{:S(2)}, u32[]{:S(2)}) async-start(f32[64,8,256]{2,1,0:T(8,128)} %bitcast.805), calls=%async_computation | async-start | bytes 1048576 | tf_op jit(solution)/shard_map/all_to_all | solution.py:36
  34.6 186.7 %all-gather.2.cloned.1.call-start = ((), (), s32[]{:S(2)}) async-start(), calls=%async_computation.2 | async-start | bytes 2129920 | tf_op jit(solution)/shard_map/all_gather | solution.py:60
  58.3 166.0 %all-to-all-start.1 = ((f32[8,64,256]{2,0,1:T(8,128)}), f32[8,64,256]{2,0,1:T(8,128)S(1)}, u32[]{:S(2)}, u32[]{:S(2)}) async-start(f32[8,64,256]{2,0,1:T(8,128)} %copy.13), calls=%async_computation.1 | async-start | bytes 1048576 | tf_op jit(solution)/shard_map/all_to_all | solution.py:50
  68.4 355.5 %all-reduce.75.cloned.1.call-start = ((), (), s32[]{:S(2)}) async-start(), calls=%async_computation.6 | async-start | bytes 1048576 | tf_op jit(solution)/shard_map/psum | solution.py:67
  221.2 6.7 copy-start
  227.1 464.8 %all-reduce.73.cloned.1.call-start = ((), (), s32[]{:S(2)}) async-start(), calls=%async_computation.5 | async-start | bytes 1048576 | tf_op jit(solution)/shard_map/psum | solution.py:67
  427.6 0.8 copy-start.3
  454.8 16.7 %copy-start.4 = (f32[256,256]{1,0:T(8,128)S(1)}, f32[256,256]{1,0:T(8,128)}, u32[]{:S(2)}) copy-start(f32[256,256]{1,0:T(8,128)} %copy-done.3) | copy-start | bytes 786436
  468.3 16.1 %copy-start.9 = (f32[256,256]{0,1:T(8,128)S(1)}, f32[256,256]{0,1:T(8,128)}, u32[]{:S(2)}) copy-start(f32[256,256]{0,1:T(8,128)} %get-tuple-element.11) | copy-start | bytes 786436
  487.2 472.7 %all-reduce.71.cloned.1.call-start = ((), (), s32[]{:S(2)}) async-start(), calls=%async_computation.4 | async-start | bytes 1048576 | tf_op jit(solution)/shard_map/psum | solution.py:67
  695.5 0.8 copy-start.5
  722.6 16.7 %copy-start.6 = (f32[256,256]{1,0:T(8,128)S(1)}, f32[256,256]{1,0:T(8,128)}, u32[]{:S(2)}) copy-start(f32[256,256]{1,0:T(8,128)} %copy-done.5) | copy-start | bytes 786436
  736.2 16.1 %copy-start.10 = (f32[256,256]{0,1:T(8,128)S(1)}, f32[256,256]{0,1:T(8,128)}, u32[]{:S(2)}) copy-start(f32[256,256]{0,1:T(8,128)} %get-tuple-element.9) | copy-start | bytes 786436
  755.1 472.8 %all-reduce.69.cloned.1.call-start = ((), (), s32[]{:S(2)}) async-start(), calls=%async_computation.3 | async-start | bytes 1048576 | tf_op jit(solution)/shard_map/psum | solution.py:67
  963.5 0.8 copy-start.7
  990.7 16.7 %copy-start.8 = (f32[256,256]{1,0:T(8,128)S(1)}, f32[256,256]{1,0:T(8,128)}, u32[]{:S(2)}) copy-start(f32[256,256]{1,0:T(8,128)} %copy-done.7) | copy-start | bytes 786436
  1004.2 16.1 %copy-start.11 = (f32[256,256]{0,1:T(8,128)S(1)}, f32[256,256]{0,1:T(8,128)}, u32[]{:S(2)}) copy-start(f32[256,256]{0,1:T(8,128)} %get-tuple-element.7) | copy-start | bytes 786436
  1231.5 0.8 copy-start.1
  1258.9 16.7 %copy-start.2 = (f32[256,256]{1,0:T(8,128)S(1)}, f32[256,256]{1,0:T(8,128)}, u32[]{:S(2)}) copy-start(f32[256,256]{1,0:T(8,128)} %copy-done.1) | copy-start | bytes 786436
  1272.4 16.1 %copy-start.12 = (f32[256,256]{0,1:T(8,128)S(1)}, f32[256,256]{0,1:T(8,128)}, u32[]{:S(2)}) copy-start(f32[256,256]{0,1:T(8,128)} %get-tuple-element.5) | copy-start | bytes 786436
Sparse Core Ops, SparseCore 0:
  41.2 179.9 all-gather.1
  227.2 196.7 all-reduce.74
  487.3 204.4 all-reduce.72
  755.2 204.6 all-reduce.70
  1023.3 204.5 all-reduce.68
where the time goes:
time: 1310 us; the launch traced here: 1300 us
  waiting for transfers between devices  979 us (75%)
  matrix products  199 us (15%)
  local copies, waits for them, and re-layouts  59 us (5%)
  starting transfers between devices  39.2 us (3%)
  between operations  14.6 us (1%)
    psum x4, waiting for transfers between devices, on_device(): gram_sum, product = lax.psum((local_gram, local_product), 'row')  805 us
    dot_general x520, matrix products, matmul(): jnp.dot(left, right, precision=lax.Precision.HIGHEST, preferred_element_t...  199 us
    all_gather x1, waiting for transfers between devices, on_device(): gathered = lax.all_gather(reflectors, 'col', axis=1, tiled=True)  153 us
    gather x64, local copies, waits for them, and re-layouts, upper_inverse(): diag_vals = jnp.diagonal(upper)  43.3 us
    all_to_all x1, starting transfers between devices, resort(): lax.all_to_all(slab_now, 'col', split_axis=0, concat_axis=1, tiled=True)  28 us
  transfers between devices with their start and end apart: 7, of which 6 were waited for; matrix products, arithmetic and copies ran while one was open for 1% of the time, Pallas kernels for 0%

commit v1 on v0

v1 whole, which is shorter than its diff:
```python
import functools

import jax
import jax.numpy as jnp
from jax import lax
from jax.experimental import pallas as pl
from jax.experimental.pallas import tpu as pltpu
from jax.sharding import PartitionSpec as P

BW = 128
BLK_DEV = 2
PANELS = 4
NY, NZH, NX = 8, 2, 4
CHIPS = 8
MESH = pl.DeviceIdType.MESH


def contract(left, right, left_dim, right_dim):
    return lax.dot_general(
        left,
        right,
        (((left_dim,), (right_dim,)), ((), ())),
        precision=lax.Precision.HIGHEST,
        preferred_element_type=jnp.float32,
    )


def matmul(left, right):
    return jnp.matmul(left, right, precision=lax.Precision.HIGHEST, preferred_element_type=jnp.float32)


def gather_kernel(pair, x_ref, o_ref, send_sem, recv_sem):
    row = lax.axis_index("row")
    col = lax.axis_index("col")
    core = lax.rem(row, 2)
    partner = row + 1 - 2 * core
    y = col // (NZH * NX)
    zh = lax.rem(col // NX, NZH)
    x = lax.rem(col, NX)
    half = x_ref.shape[-1] // 2

    def device(yy, zz, xx):
        return (row, (yy * NZH + zz) * NX + xx)

    up_y, down_y = lax.rem(y + 1, NY), lax.rem(y + NY - 1, NY)
    up_x, down_x = lax.rem(x + 1, NX), lax.rem(x + NX - 1, NX)
    across = device(y, 1 - zh, x)
    greeted = [device(up_y, zh, x), device(down_y, zh, x), device(y, zh, up_x), device(y, zh, down_x), across]
    if pair:
        greeted.append((partner, col))
    barrier = pltpu.get_barrier_semaphore()
    for other in greeted:
        pl.semaphore_signal(barrier, inc=1, device_id=other, device_id_type=MESH)
    pl.semaphore_wait(barrier, len(greeted))

    def spot(yy, zz, xx, h):
        lanes = slice(None) if h is None else pl.ds(h * half, half)
        middle = (core,) if pair else ()
        return o_ref.at[(yy, zz, xx) + middle + (slice(None), lanes)]

    sent = []
    counter = [0]

    def launch(source, target, number, to):
        copy = pltpu.make_async_remote_copy(
            src_ref=source,
            dst_ref=target,
            send_sem=send_sem.at[number],
            recv_sem=recv_sem.at[number],
            device_id=to,
            device_id_type=MESH,
        )
        copy.start()
        sent.append(copy)

    def arrived(target, number, origin):
        pltpu.make_async_remote_copy(
            src_ref=target,
            dst_ref=target,
            send_sem=send_sem.at[number],
            recv_sem=recv_sem.at[number],
            device_id=origin,
            device_id_type=MESH,
        ).wait_recv()

    def number():
        counter[0] += 1
        return counter[0] - 1

    everything = slice(None)

    def ring(length, place, region, first, to_device, flip):
        sign = -1 if flip else 1
        pending = []
        for hop in range(1, length // 2 + 1):
            for origin_at, origin_number, origin_from in pending:
                arrived(origin_at, origin_number, origin_from)
            pending = []
            for way in (1, -1):
                if way == -1 and hop == length // 2:
                    continue
                step = way * sign
                ahead = lax.rem(place + step + length, length)
                behind = lax.rem(place - step + length, length)
                carried = lax.rem(place - step * (hop - 1) + length * 4, length)
                coming = lax.rem(place - step * hop + length * 4, length)
                mark = number()
                source = first if (hop == 1 and first is not None) else region(carried)
                launch(source, region(carried), mark, to_device(ahead))
                pending.append((region(coming), mark, to_device(behind)))
            yield
        for origin_at, origin_number, origin_from in pending:
            arrived(origin_at, origin_number, origin_from)

    def stream(h, zz, own):
        lanes = pl.ds(h * half, half)
        first = x_ref.at[:, lanes] if own else None
        x_device = lambda p: device(y, zh, p)
        y_device = lambda p: device(p, zh, x)
        if h == 0:
            yield from ring(NX, x, lambda p: spot(y, zz, p, h), first, x_device, False)
            yield from ring(NY, y, lambda p: spot(p, zz, everything, h), None, y_device, False)
        else:
            yield from ring(NY, y, lambda p: spot(p, zz, x, h), first, y_device, True)
            yield from ring(NX, x, lambda p: spot(everything, zz, p, h), None, x_device, True)

    mark_across = number()
    launch(x_ref, spot(y, zh, x, None), mark_across, across)
    early = [stream(0, zh, True), stream(1, zh, True)]
    late = [stream(0, 1 - zh, False), stream(1, 1 - zh, False)]

    def advance(streams):
        for one in streams:
            next(one, None)

    advance(early)
    if pair:
        o_ref[y, zh, x, core] = x_ref[...]
    else:
        o_ref[y, zh, x] = x_ref[...]
    for _ in range(3):
        advance(early)
    arrived(spot(y, 1 - zh, x, None), mark_across, across)
    advance(late)
    advance(early)
    advance(late)
    advance(early)
    advance(late)
    advance(early)
    for _ in range(4):
        advance(late)
    if pair:
        mark_pair = number()
        launch(o_ref.at[:, :, :, core], o_ref.at[:, :, :, core], mark_pair, (partner, col))
        other = o_ref.at[:, :, :, 1 - core]
        arrived(other, mark_pair, (partner, col))
    for copy in sent:
        copy.wait_send()


def gather_col(block, pair, collective_id):
    rows, lanes = block.shape
    shape = (NY, NZH, NX) + ((2,) if pair else ()) + (rows, lanes)
    copies = 1 + 4 * (NX - 1 + NY - 1) + (1 if pair else 0)
    return pl.pallas_call(
        functools.partial(gather_kernel, pair),
        out_shape=jax.ShapeDtypeStruct(shape, block.dtype),
        in_specs=[pl.BlockSpec(memory_space=pltpu.VMEM)],
        out_specs=pl.BlockSpec(memory_space=pltpu.VMEM),
        scratch_shapes=[pltpu.SemaphoreType.DMA((copies,)), pltpu.SemaphoreType.DMA((copies,))],
        compiler_params=pltpu.CompilerParams(collective_id=collective_id, has_side_effects=True),
        name="gather_pair" if pair else "gather_rows",
    )(block)


def reduce_kernel(pair, subs, x_ref, o_ref, acc, from_left, from_right, swap, ssem, rsem):
    row = lax.axis_index("row")
    col = lax.axis_index("col")
    core = lax.rem(row, 2)
    me = row // 2
    partner = (row + 1 - 2 * core, col)
    right = (jnp.minimum(row + 2, 2 * CHIPS - 2 + core), col)
    left = (jnp.maximum(row - 2, core), col)
    has_left, has_right = me > 0, me < CHIPS - 1
    rows, lanes = acc.shape
    by_rows = rows >= 8 * CHIPS
    piece = rows // CHIPS // subs if by_rows else lanes // CHIPS // subs

    def part(j, q):
        start = (j * subs + q) * piece
        if by_rows:
            return (pl.ds(pl.multiple_of(start, 8), piece), slice(None))
        return (slice(None), pl.ds(pl.multiple_of(start, 128), piece))

    barrier = pltpu.get_barrier_semaphore()
    pl.semaphore_signal(barrier, inc=1, device_id=partner, device_id_type=MESH)

    @pl.when(has_left)
    def _():
        pl.semaphore_signal(barrier, inc=1, device_id=left, device_id_type=MESH)

    @pl.when(has_right)
    def _():
        pl.semaphore_signal(barrier, inc=1, device_id=right, device_id_type=MESH)

    pl.semaphore_wait(barrier, 1 + has_left.astype(jnp.int32) + has_right.astype(jnp.int32))

    def copy(source, target, kind, j, q, to):
        return pltpu.make_async_remote_copy(
            src_ref=source,
            dst_ref=target,
            send_sem=ssem.at[kind, j, q],
            recv_sem=rsem.at[kind, j, q],
            device_id=to,
            device_id_type=MESH,
        )

    def swap_copy(j, q):
        return copy(x_ref.at[(1 - core,) + part(j, q)], swap.at[part(j, q)], 0, j, q, partner)

    def rightward(j, q):
        return copy(from_left.at[part(j, q)], from_left.at[part(j, q)], 1, j, q, right)

    def leftward(j, q):
        return copy(from_right.at[part(j, q)], from_right.at[part(j, q)], 2, j, q, left)

    def out_right(j, q):
        return copy(o_at(j, q), o_at(j, q), 3, j, q, right)

    def out_left(j, q):
        return copy(o_at(j, q), o_at(j, q), 4, j, q, left)

    def out_pair(j, q):
        return copy(o_at(j, q), o_at(j, q), 5, j, q, partner)

    def other_pair(j, q):
        there = o_ref.at[(1 - core,) + part(j, q)]
        return copy(there, there, 5, j, q, partner)

    def o_at(j, q):
        return o_ref.at[(core,) + part(j, q)] if pair else o_ref.at[part(j, q)]

    order = []
    for k in range(CHIPS // 2):
        order += [CHIPS - 1 - k, k]
    for j in order:
        for q in range(subs):
            swap_copy(j, q).start()
    for j in order:
        for q in range(subs):
            swap_copy(j, q).wait_recv()
            at = part(j, q)
            acc[at] = x_ref[(core,) + at] + swap[at]

    def inward(s, _):
        for q in range(subs):

            @pl.when(jnp.logical_and(s >= me, has_right))
            def _():
                j = me + CHIPS - 1 - s
                at = part(j, q)

                @pl.when(has_left)
                def _():
                    rightward(j, q).wait_recv()
                    from_left[at] = from_left[at] + acc[at]

                @pl.when(jnp.logical_not(has_left))
                def _():
                    from_left[at] = acc[at]

                rightward(j, q).start()

            @pl.when(jnp.logical_and(s >= CHIPS - 1 - me, has_left))
            def _():
                j = me - (CHIPS - 1) + s
                at = part(j, q)

                @pl.when(has_right)
                def _():
                    leftward(j, q).wait_recv()
                    from_right[at] = from_right[at] + acc[at]

                @pl.when(jnp.logical_not(has_right))
                def _():
                    from_right[at] = acc[at]

                leftward(j, q).start()

        return 0

    lax.fori_loop(0, CHIPS - 1, inward, 0)

    for q in range(subs):
        at = part(me, q)

        @pl.when(has_left)
        def _():
            rightward(me, q).wait_recv()
            acc[at] = acc[at] + from_left[at]

        @pl.when(has_right)
        def _():
            leftward(me, q).wait_recv()
            acc[at] = acc[at] + from_right[at]

        if pair:
            o_ref[(core,) + at] = acc[at]
        else:
            o_ref[at] = acc[at]

    def outward(s, _):
        for q in range(subs):

            @pl.when(s <= me)
            def _():
                j = me - s

                @pl.when(s > 0)
                def _():
                    out_right(j, q).wait_recv()

                @pl.when(has_right)
                def _():
                    out_right(j, q).start()

                if pair:
                    out_pair(j, q).start()

            @pl.when(s <= CHIPS - 1 - me)
            def _():
                j = me + s

                @pl.when(s > 0)
                def _():
                    out_left(j, q).wait_recv()
                    if pair:
                        out_pair(j, q).start()

                @pl.when(has_left)
                def _():
                    out_left(j, q).start()

        return 0

    lax.fori_loop(0, CHIPS, outward, 0)

    def finish(j, _):
        for q in range(subs):
            swap_copy(j, q).wait_send()

            @pl.when(jnp.logical_and(has_right, j > me))
            def _():
                rightward(j, q).wait_send()

            @pl.when(jnp.logical_and(has_left, j < me))
            def _():
                leftward(j, q).wait_send()

            @pl.when(jnp.logical_and(has_right, j <= me))
            def _():
                out_right(j, q).wait_send()

            @pl.when(jnp.logical_and(has_left, j >= me))
            def _():
                out_left(j, q).wait_send()

            if pair:
                out_pair(j, q).wait_send()
                other_pair(j, q).wait_recv()
        return 0

    lax.fori_loop(0, CHIPS, finish, 0)


def reduce_row(halves, pair, subs, collective_id):
    _, rows, lanes = halves.shape
    shape = (2, rows, lanes) if pair else (rows, lanes)
    half = pltpu.VMEM((rows, lanes), halves.dtype)
    kinds = 6 if pair else 5
    return pl.pallas_call(
        functools.partial(reduce_kernel, pair, subs),
        out_shape=jax.ShapeDtypeStruct(shape, halves.dtype),
        in_specs=[pl.BlockSpec(memory_space=pltpu.VMEM)],
        out_specs=pl.BlockSpec(memory_space=pltpu.VMEM),
        scratch_shapes=[
            half,
            half,
            half,
            half,
            pltpu.SemaphoreType.DMA((kinds, CHIPS, subs)),
            pltpu.SemaphoreType.DMA((kinds, CHIPS, subs)),
        ],
        compiler_params=pltpu.CompilerParams(collective_id=collective_id, has_side_effects=True),
        name="sum_pair" if pair else "sum_half",
    )(halves)


def scaled_inverses(diag_blocks):
    order = diag_blocks.shape[-1]
    at_row = lax.broadcasted_iota(jnp.int32, (order, order), 0)
    at_col = lax.broadcasted_iota(jnp.int32, (order, order), 1)
    halves = 0.5 * jnp.sum(jnp.where(at_row == at_col, diag_blocks, 0.0), axis=2)
    strict = jnp.where(at_row < at_col, -diag_blocks / halves[:, :, None], 0.0)
    size = 16
    power = jnp.where(at_row // size == at_col // size, strict, 0.0)
    inverse = jnp.where(at_row == at_col, 1.0, power)
    for _ in range(3):
        power = matmul(power, power)
        inverse = inverse + matmul(inverse, power)
    while size < order:
        corner = jnp.where(
            jnp.logical_and(at_row // (2 * size) == at_col // (2 * size), at_row // size != at_col // size), strict, 0.0
        )
        inverse = inverse + matmul(matmul(inverse, corner), inverse)
        size *= 2
    return inverse, 1.0 / halves


def times_inverse(panel_rows, gram):
    order = gram.shape[0] // PANELS
    cut = lambda p: slice(p * order, (p + 1) * order)
    inverse, scale = scaled_inverses(jnp.stack([gram[cut(p), cut(p)] for p in range(PANELS)]))
    done = []
    for p in range(PANELS):
        rest = panel_rows[:, cut(p)]
        if p:
            rest = rest - matmul(jnp.concatenate(done, axis=1), gram[: p * order, cut(p)])
        done.append(matmul(rest, inverse[p]) * scale[p][None, :])
    return jnp.concatenate(done, axis=1)


def resort(slab_now, owner_list, slot_list):
    spread = lax.all_to_all(slab_now, "col", split_axis=0, concat_axis=1, tiled=True)
    blocks = owner_list.shape[0]
    target = owner_list * BLK_DEV + slot_list
    positions = jnp.arange(blocks, dtype=jnp.int32)
    one_hot = (target[:, None] == positions[None, :]).astype(jnp.float32)
    blocks_view = spread.reshape(spread.shape[0], blocks, BW)
    ordered = jnp.einsum(
        "rbw,bc->rcw",
        blocks_view,
        one_hot,
        precision=lax.Precision.HIGHEST,
        preferred_element_type=jnp.float32,
    )
    ordered = ordered.reshape(spread.shape[0], blocks * BW)
    return lax.all_to_all(ordered, "col", split_axis=1, concat_axis=0, tiled=True)


def on_device(vectors, reflectors, owner_list, slot_list):
    panels, rows, width = reflectors.shape
    order = panels * width
    col = lax.axis_index("col")
    own_rows = jnp.transpose(reflectors, (1, 0, 2)).reshape(rows, order)
    panel_rows = gather_col(own_rows, False, 0).reshape(NY * NZH * NX * rows, order)
    slab_now = resort(vectors, owner_list, slot_list)
    share = order // (NY * NZH * NX)
    own_columns = lax.dynamic_slice_in_dim(panel_rows, col * share, share, axis=1)
    gram_part = contract(own_columns, panel_rows, 0, 0)
    gram_half = reduce_row(gram_part.reshape(2, share // 2, order), False, 1, 1)
    gram = gather_col(gram_half, True, 2).reshape(order, order)
    product_part = contract(slab_now, panel_rows, 0, 0)
    columns = product_part.shape[0]
    product = reduce_row(product_part.reshape(2, columns // 2, order), True, 2, 3).reshape(columns, order)
    mixed = times_inverse(panel_rows, gram)
    return slab_now - contract(mixed, product, 1, 1)


def solution(mesh):
    return jax.shard_map(
        on_device,
        mesh=mesh,
        in_specs=(P("row", "col"), P(None, ("row", "col"), None), P(), P()),
        out_specs=P("row", "col"),
        check_vma=False,
    )
```

time: 1310 us -> 328 us (0.25)
  waiting for transfers between devices: 979 us -> 15.1 us
  Pallas kernels: 0 us -> 208 us
  matrix products: 199 us -> 46.6 us
  local copies, waits for them, and re-layouts: 59 us -> 6.75 us
  between operations: 14.6 us -> 0.63 us
    psum x4 -> x0, waiting for transfers between devices: 805 us -> none  [on_device(): gram_sum, product = lax.psum((local_gram, local_product), 'row')]
    pallas_call x0 -> x4, Pallas kernels: none -> 208 us  [the longest x2 106 us: gather_col(): pl.pallas_call(functools.partial(gather_kernel, pair), out_shape=jax.Shap...]
    all_gather x1 -> x0, waiting for transfers between devices: 153 us -> none  [on_device(): gathered = lax.all_gather(reflectors, 'col', axis=1, tiled=True)]
    dot_general x520 -> x24, matrix products: 199 us -> 46.2 us  [the longest x21 33.4 us: matmul(): jnp.matmul(left, right, precision=lax.Precision.HIGHEST, preferred_elemen...]
    gather x68 -> x0, local copies, waits for them, and re-layouts: 53.6 us -> none  [the longest x64 43.3 us: upper_inverse(): diag_vals = jnp.diagonal(upper)]
    all_to_all x1, waiting for transfers between devices: 20.5 us -> 0.01 us  [resort(): lax.all_to_all(slab_now, 'col', split_axis=0, concat_axis=1, tiled=True)]
    all_to_all x1, waiting for transfers between devices: 0.01 us -> 15.1 us  [resort(): lax.all_to_all(ordered, 'col', split_axis=1, concat_axis=0, tiled=True)]
  transfers between devices with their start and end apart: 7 -> 2, of which waited for: 6 -> 1; matrix products, arithmetic and copies ran while one was open for 1% -> 13% of each run, Pallas kernels for 0% -> 47%
where the time goes in v1:
time: 328 us; the launch traced here: 323 us
  Pallas kernels  208 us (63%)
  matrix products  46.6 us (14%)
  starting transfers between devices  45 us (14%)
  waiting for transfers between devices  15.1 us (5%)
  local copies, waits for them, and re-layouts  6.75 us (2%)
    pallas_call x2, Pallas kernels, gather_col(): pl.pallas_call(functools.partial(gather_kernel, pair), out_shape=jax.Shap...  106 us
    pallas_call x2, Pallas kernels, reduce_row(): pl.pallas_call(functools.partial(reduce_kernel, pair, subs), out_shape=ja...  102 us
    dot_general x21, matrix products, matmul(): jnp.matmul(left, right, precision=lax.Precision.HIGHEST, preferred_elemen...  33.4 us
    all_to_all x1, starting transfers between devices, resort(): lax.all_to_all(slab_now, 'col', split_axis=0, concat_axis=1, tiled=True)  28 us
    all_to_all x1, starting transfers between devices, resort(): lax.all_to_all(ordered, 'col', split_axis=1, concat_axis=0, tiled=True)  17 us
    all_to_all x1, waiting for transfers between devices, resort(): lax.all_to_all(ordered, 'col', split_axis=1, concat_axis=0, tiled=True)  15.1 us
    dot_general x3, matrix products, contract(): lax.dot_general(left, right, (((left_dim,), (right_dim,)), ((), ())), pre...  12.8 us
  transfers between devices with their start and end apart: 2, of which 1 were waited for; matrix products, arithmetic and copies ran while one was open for 13% of the time, Pallas kernels for 47%

profile of v1, /device:TPU:1, one launch (start us, length us, event | category | flops | bytes accessed | tf_op | source)
XLA Modules:
  0.0 323.4 jit_solution(13228430384527431102)
XLA Ops:
  0.0 28.0 %all-to-all-start = ((f32[64,8,256]{2,1,0:T(8,128)}), f32[64,8,256]{2,1,0:T(8,128)S(1)}, u32[]{:S(2)}, u32[]{:S(2)}) async-start(f32[64,8,256]{2,1,0:T(8,128)} %bitcast.99), calls=%async_computation | async-start | bytes 1048576 | tf_op jit(solution)/shard_map/all_to_all | solution.py:434
  28.2 48.3 %gather_rows.1 = f32[8,2,4,8,1024]{4,3,2,1,0:T(8,128)} custom-call(f32[8,1024]{1,0:T(8,128)} %bitcast.100), custom_call_target="tpu_custom_call" | custom-call | tf_op jit(solution)/shard_map/gather_rows/pallas_call | solution.py:165
  77.7 3.3 %fusion.59.x_ref = f32[2,8,1024]{2,1,0:T(8,128)} fusion(f32[512,1024,1]{1,0,2:T(8,128)} %bitcast.83, f32[16,512]{1,0:T(8,128)S(1)} %copy.11), kind=kOutput, calls=%fused_computation.92 | convolution fusion | flops 100663296 | bytes 2195456 | tf_op jit(solution)/shard_map/dot_general | solution.py:19
  81.0 47.0 %sum_half.1.x_ref = f32[8,1024]{1,0:T(8,128)} custom-call(f32[2,8,1024]{2,1,0:T(8,128)} %fusion.59.x_ref), custom_call_target="tpu_custom_call" | custom-call | tf_op jit(solution)/shard_map/sum_half/pallas_call | solution.py:381
  128.0 57.4 %gather_pair.1 = f32[8,2,4,2,8,1024]{5,4,3,2,1,0:T(8,128)} custom-call(f32[8,1024]{1,0:T(8,128)} %sum_half.1.x_ref), custom_call_target="tpu_custom_call" | custom-call | tf_op jit(solution)/shard_map/gather_pair/pallas_call | solution.py:165
  185.5 1.3 slice_bitcast_fusion.11
  188.0 1.7 fusion.32
  189.7 1.5 convolution_add_fusion.6
  195.9 1.4 fusion.29
  198.6 1.4 fusion.27
  200.0 1.7 convolution_add_fusion.2
  201.7 1.4 fusion.25
  204.4 2.4 fusion.23
  208.7 17.0 %all-to-all-start.1 = ((f32[8,64,256]{2,0,1:T(8,128)}), f32[8,64,256]{2,0,1:T(8,128)}, u32[]{:S(2)}, u32[]{:S(2)}) async-start(f32[8,64,256]{2,0,1:T(8,128)} %copy.10), calls=%async_computation.1 | async-start | bytes 1048576 | tf_op jit(solution)/shard_map/all_to_all | solution.py:448
  225.6 2.4 convolution_add_fusion
  229.1 2.0 convolution_subtract_fusion.1
  231.7 2.9 convolution_subtract_fusion
  236.1 3.8 %fusion.17 = f32[512,256]{1,0:T(8,128)S(1)} fusion(f32[512,256]{0,1:T(8,128)S(1)} %convolution_multiply_fusion.1, f32[512,256]{0,1:T(8,128)S(1)} %convolution_multiply_fusion.2, f32[512,256]{0,1:T(8,128)S(1)} %bitcast.94, f32[1024,1024]{1,0:T(8,128)} %bitcast.92, f32[512,1024]{1,0:T(8,128)S(1)} %bitcast.87), kind=kOutput, calls=%fused_computation.24 | convolution fusion | flops 1208877056 | bytes 3407872 | tf_op jit(solution)/shard_map/dot_general | solution.py:29
  239.9 1.5 convolution_multiply_fusion
  241.3 15.1 %all-to-all-done.1 = f32[8,64,256]{2,0,1:T(8,128)} async-done(((f32[8,64,256]{2,0,1:T(8,128)}), f32[8,64,256]{2,0,1:T(8,128)}, u32[]{:S(2)}, u32[]{:S(2)}) %all-to-all-start.1) | async-done | bytes 524320 | tf_op jit(solution)/shard_map/all_to_all | solution.py:448
  256.4 2.0 copy.12
  258.5 3.9 %fusion.76.x_ref = f32[2,128,1024]{2,1,0:T(8,128)} fusion(f32[2,128,512]{2,1,0:T(8,128)} %bitcast.96, f32[512,1024,1]{1,0,2:T(8,128)S(1)} %bitcast.88), kind=kOutput, calls=%fused_computation.133 | convolution fusion | flops 1610612736 | bytes 3670016 | tf_op jit(solution)/shard_map/dot_general | solution.py:19
  262.4 55.2 %sum_pair.1 = f32[2,128,1024]{2,1,0:T(8,128)} custom-call(f32[2,128,1024]{2,1,0:T(8,128)} %fusion.76.x_ref), custom_call_target="tpu_custom_call" | custom-call | tf_op jit(solution)/shard_map/sum_pair/pallas_call | solution.py:381
  317.6 5.6 %fusion.14 = f32[512,256]{1,0:T(8,128)} fusion(f32[256,1024]{1,0:T(8,128)} %bitcast.98, f32[512,256]{0,1:T(8,128)S(1)} %copy-done.3, f32[512,256]{0,1:T(8,128)S(1)} %copy-done.2, f32[512,256]{0,1:T(8,128)S(1)} %convolution_multiply_fusion.2, f32[512,256]{0,1:T(8,128)S(1)} %bitcast.95, f32[8,64,256]{2,0,1:T(8,128)} %all-to-all-done.1), kind=kOutput, calls=%fused_computation.22 | convolution fusion | flops 1612316672 | bytes 4194304 | tf_op jit(solution)/shard_map/dot_general | solution.py:19
  (43 shorter events, 14.6 us)
Async XLA Ops:
  0.0 206.8 %all-to-all-start = ((f32[64,8,256]{2,1,0:T(8,128)}), f32[64,8,256]{2,1,0:T(8,128)S(1)}, u32[]{:S(2)}, u32[]{:S(2)}) async-start(f32[64,8,256]{2,1,0:T(8,128)} %bitcast.99), calls=%async_computation | async-start | bytes 1048576 | tf_op jit(solution)/shard_map/all_to_all | solution.py:434
  195.9 1.5 copy-start.4
  195.9 1.5 copy-start.5
  208.7 19.4 %copy-start = (f32[8,2,4,8,1024]{4,3,2,1,0:T(8,128)S(1)}, f32[8,2,4,8,1024]{4,3,2,1,0:T(8,128)}, u32[]{:S(2)}) copy-start(f32[8,2,4,8,1024]{4,3,2,1,0:T(8,128)} %gather_rows.1) | copy-start | bytes 6291460
  208.7 47.8 %all-to-all-start.1 = ((f32[8,64,256]{2,0,1:T(8,128)}), f32[8,64,256]{2,0,1:T(8,128)}, u32[]{:S(2)}, u32[]{:S(2)}) async-start(f32[8,64,256]{2,0,1:T(8,128)} %copy.10), calls=%async_computation.1 | async-start | bytes 1048576 | tf_op jit(solution)/shard_map/all_to_all | solution.py:448
  235.3 0.8 copy-start.1
  262.4 55.2 %copy-start.2 = (f32[512,256]{0,1:T(8,128)S(1)}, f32[512,256]{0,1:T(8,128)}, u32[]{:S(2)}) copy-start(f32[512,256]{0,1:T(8,128)} %copy-done.1) | copy-start | bytes 1572868
  262.4 55.2 %copy-start.3 = (f32[512,256]{0,1:T(8,128)S(1)}, f32[512,256]{0,1:T(8,128)}, u32[]{:S(2)}) copy-start(f32[512,256]{0,1:T(8,128)} %convolution_multiply_fusion) | copy-start | bytes 1572868

commit v2 on v1

v2 whole, which is shorter than its diff:
```python
import functools

import jax
import jax.numpy as jnp
from jax import lax
from jax.experimental import pallas as pl
from jax.experimental.pallas import tpu as pltpu
from jax.sharding import PartitionSpec as P

BW = 128
BLK_DEV = 2
PANELS = 4
NY, NZH, NX = 8, 2, 4
CHIPS = 8
MESH = pl.DeviceIdType.MESH
VMEM = pl.BlockSpec(memory_space=pltpu.VMEM)


def contract(left, right, left_dim, right_dim, precision=lax.Precision.HIGH):
    return lax.dot_general(
        left,
        right,
        (((left_dim,), (right_dim,)), ((), ())),
        precision=precision,
        preferred_element_type=jnp.float32,
    )


def matmul(left, right):
    return jnp.matmul(left, right, precision=lax.Precision.HIGH, preferred_element_type=jnp.float32)


def greet(always, sometimes):
    barrier = pltpu.get_barrier_semaphore()
    count = len(always)
    for other in always:
        pl.semaphore_signal(barrier, inc=1, device_id=other, device_id_type=MESH)
    for flag, other in sometimes:

        @pl.when(flag)
        def _():
            pl.semaphore_signal(barrier, inc=1, device_id=other, device_id_type=MESH)

        count = count + flag.astype(jnp.int32)
    pl.semaphore_wait(barrier, count)


def place_in_col(col):
    return col // (NZH * NX), lax.rem(col // NX, NZH), lax.rem(col, NX)


def gather_peers(row, col):
    y, zh, x = place_in_col(col)
    at = lambda yy, zz, xx: (row, (yy * NZH + zz) * NX + xx)
    peers = [at(lax.rem(y + d, NY), zh, x) for d in range(1, NY)]
    peers += [at(y, zh, lax.rem(x + d, NX)) for d in range(1, NX)]
    return peers + [at(y, 1 - zh, x)]


def gather_steps(pair, x_ref, o_ref, send_sem, recv_sem):
    row = lax.axis_index("row")
    col = lax.axis_index("col")
    core = lax.rem(row, 2)
    partner = (row + 1 - 2 * core, col)
    y, zh, x = place_in_col(col)
    quarter = x_ref.shape[-1] // 4
    lanes_of = (pl.ds(0, quarter), pl.ds(quarter, 3 * quarter))
    sent = []
    everything = slice(None)

    def device(yy, zz, xx):
        return (row, (yy * NZH + zz) * NX + xx)

    def spot(yy, zz, xx, lanes):
        middle = (core,) if pair else ()
        return o_ref.at[(yy, zz, xx) + middle + (everything, lanes)]

    def launch(source, target, to):
        number = len(sent)
        copy = pltpu.make_async_remote_copy(
            src_ref=source,
            dst_ref=target,
            send_sem=send_sem.at[number],
            recv_sem=recv_sem.at[number],
            device_id=to,
            device_id_type=MESH,
        )
        copy.start()
        sent.append(copy)
        return number

    def arrived(target, number, origin):
        pltpu.make_async_remote_copy(
            src_ref=target,
            dst_ref=target,
            send_sem=send_sem.at[number],
            recv_sem=recv_sem.at[number],
            device_id=origin,
            device_id_type=MESH,
        ).wait_recv()

    def spread(length, place, region, first, to_device):
        waits = []
        for d in sorted(range(1, length), key=lambda d: -min(d, length - d)):
            ahead = lax.rem(place + d, length)
            behind = lax.rem(place + length - d, length)
            number = launch(region(place) if first is None else first, region(place), to_device(ahead))
            waits.append((region(behind), number, to_device(behind)))
        return waits

    def finish(waits):
        for target, number, origin in waits:
            arrived(target, number, origin)

    def by_y(zz, xx, part, first):
        return spread(NY, y, lambda p: spot(p, zz, xx, lanes_of[part]), first, lambda p: device(p, zh, x))

    def by_x(zz, yy, part, first):
        return spread(NX, x, lambda p: spot(yy, zz, p, lanes_of[part]), first, lambda p: device(y, zh, p))

    whole = slice(None)
    across = launch(x_ref, spot(y, zh, x, whole), device(y, 1 - zh, x))
    near_y = by_y(zh, x, 1, x_ref.at[:, lanes_of[1]])
    near_x = by_x(zh, y, 0, x_ref.at[:, lanes_of[0]])
    if pair:
        o_ref[y, zh, x, core] = x_ref[...]
    else:
        o_ref[y, zh, x] = x_ref[...]
    yield
    finish(near_y)
    wide_x = by_x(zh, everything, 1, None)
    finish(near_x)
    wide_y = by_y(zh, everything, 0, None)
    yield
    far = 1 - zh
    arrived(spot(y, far, x, whole), across, device(y, far, x))
    far_y = by_y(far, x, 1, None)
    far_x = by_x(far, y, 0, None)
    yield
    finish(far_y)
    far_wide_x = by_x(far, everything, 1, None)
    finish(far_x)
    far_wide_y = by_y(far, everything, 0, None)
    yield
    finish(wide_x)
    finish(wide_y)

    def half_of(zz, cc):
        return o_ref.at[:, zz, :, cc]

    if pair:
        first_swap = launch(half_of(zh, core), half_of(zh, core), partner)
    yield
    finish(far_wide_x)
    finish(far_wide_y)
    if pair:
        second_swap = launch(half_of(far, core), half_of(far, core), partner)
        yield
        arrived(half_of(zh, 1 - core), first_swap, partner)
        arrived(half_of(far, 1 - core), second_swap, partner)
    for copy in sent:
        copy.wait_send()


def gather_copies(pair):
    return 1 + 4 * (NX - 1 + NY - 1) + (2 if pair else 0)


def line_places(row, col):
    core = lax.rem(row, 2)
    right = (jnp.minimum(row + 2, 2 * CHIPS - 2 + core), col)
    left = (jnp.maximum(row - 2, core), col)
    return row // 2, core, (row + 1 - 2 * core, col), left, right


def reduce_steps(subs, x_ref, o_ref, acc, from_left, from_right, swap, ssem, rsem):
    me, core, partner, left, right = line_places(lax.axis_index("row"), lax.axis_index("col"))
    has_left, has_right = me > 0, me < CHIPS - 1
    piece = acc.shape[0] // CHIPS // subs

    def part(j, q):
        return (pl.ds(pl.multiple_of((j * subs + q) * piece, 8), piece), slice(None))

    def copy(source, target, kind, j, q, to):
        return pltpu.make_async_remote_copy(
            src_ref=source,
            dst_ref=target,
            send_sem=ssem.at[kind, j, q],
            recv_sem=rsem.at[kind, j, q],
            device_id=to,
            device_id_type=MESH,
        )

    def swap_copy(j, q):
        return copy(x_ref.at[(1 - core,) + part(j, q)], swap.at[part(j, q)], 0, j, q, partner)

    def rightward(j, q):
        return copy(from_left.at[part(j, q)], from_left.at[part(j, q)], 1, j, q, right)

    def leftward(j, q):
        return copy(from_right.at[part(j, q)], from_right.at[part(j, q)], 2, j, q, left)

    def o_at(j, q):
        return o_ref.at[(core,) + part(j, q)]

    def out_right(j, q):
        return copy(o_at(j, q), o_at(j, q), 3, j, q, right)

    def out_left(j, q):
        return copy(o_at(j, q), o_at(j, q), 4, j, q, left)

    def out_pair(j, q):
        return copy(o_at(j, q), o_at(j, q), 5, j, q, partner)

    def other_pair(j, q):
        there = o_ref.at[(1 - core,) + part(j, q)]
        return copy(there, there, 5, j, q, partner)

    order = []
    for k in range(CHIPS // 2):
        order += [CHIPS - 1 - k, k]
    for j in order:
        for q in range(subs):
            swap_copy(j, q).start()
    yield
    for j in order:
        for q in range(subs):
            swap_copy(j, q).wait_recv()
            at = part(j, q)
            acc[at] = x_ref[(core,) + at] + swap[at]

    for s in range(CHIPS - 1):
        for q in range(subs):

            @pl.when(jnp.logical_and(me <= s, has_right))
            def _():
                j = me + CHIPS - 1 - s
                at = part(j, q)

                @pl.when(has_left)
                def _():
                    rightward(j, q).wait_recv()
                    from_left[at] = from_left[at] + acc[at]

                @pl.when(jnp.logical_not(has_left))
                def _():
                    from_left[at] = acc[at]

                rightward(j, q).start()

            @pl.when(jnp.logical_and(me >= CHIPS - 1 - s, has_left))
            def _():
                j = me - (CHIPS - 1) + s
                at = part(j, q)

                @pl.when(has_right)
                def _():
                    leftward(j, q).wait_recv()
                    from_right[at] = from_right[at] + acc[at]

                @pl.when(jnp.logical_not(has_right))
                def _():
                    from_right[at] = acc[at]

                leftward(j, q).start()

        yield

    for q in range(subs):
        at = part(me, q)

        @pl.when(has_left)
        def _():
            rightward(me, q).wait_recv()
            acc[at] = acc[at] + from_left[at]

        @pl.when(has_right)
        def _():
            leftward(me, q).wait_recv()
            acc[at] = acc[at] + from_right[at]

        o_ref[(core,) + at] = acc[at]

    for s in range(CHIPS):
        for q in range(subs):

            @pl.when(me >= s)
            def _():
                j = me - s
                if s:
                    out_right(j, q).wait_recv()

                @pl.when(has_right)
                def _():
                    out_right(j, q).start()

                out_pair(j, q).start()

            @pl.when(me <= CHIPS - 1 - s)
            def _():
                j = me + s
                if s:
                    out_left(j, q).wait_recv()
                    out_pair(j, q).start()

                @pl.when(has_left)
                def _():
                    out_left(j, q).start()

        yield

    def finish(j, _):
        for q in range(subs):
            swap_copy(j, q).wait_send()

            @pl.when(jnp.logical_and(has_right, j > me))
            def _():
                rightward(j, q).wait_send()

            @pl.when(jnp.logical_and(has_left, j < me))
            def _():
                leftward(j, q).wait_send()

            @pl.when(jnp.logical_and(has_right, j <= me))
            def _():
                out_right(j, q).wait_send()

            @pl.when(jnp.logical_and(has_left, j >= me))
            def _():
                out_left(j, q).wait_send()

            out_pair(j, q).wait_send()
            other_pair(j, q).wait_recv()
        return 0

    lax.fori_loop(0, CHIPS, finish, 0)


def rows_kernel(x_ref, o_ref, ssem, rsem):
    greet(gather_peers(lax.axis_index("row"), lax.axis_index("col")), [])
    for _ in gather_steps(False, x_ref, o_ref, ssem, rsem):
        pass


def short_sum_kernel(x_ref, o_ref, acc, swap, got, ssem, rsem):
    row = lax.axis_index("row")
    col = lax.axis_index("col")
    core = lax.rem(row, 2)
    me = row // 2
    partner = (row + 1 - 2 * core, col)
    on_line = lambda k: (2 * k + core, col)
    ahead = lambda d: lax.rem(me + d, CHIPS)
    behind = lambda d: lax.rem(me + CHIPS - d, CHIPS)
    lanes = acc.shape[1] // CHIPS
    chunk = lambda j: (slice(None), pl.ds(pl.multiple_of(j * lanes, lanes), lanes))
    order = list(range(1, CHIPS))
    greet([partner] + [on_line(ahead(d)) for d in order], [])

    def copy(source, target, number, to):
        return pltpu.make_async_remote_copy(
            src_ref=source,
            dst_ref=target,
            send_sem=ssem.at[number],
            recv_sem=rsem.at[number],
            device_id=to,
            device_id_type=MESH,
        )

    first = copy(x_ref.at[1 - core], swap, 0, partner)
    first.start()
    first.wait_recv()
    acc[...] = x_ref[core] + swap[...]
    inward = [copy(acc.at[chunk(ahead(d))], got.at[me], d, on_line(ahead(d))) for d in order]
    for one in inward:
        one.start()
    total = acc[chunk(me)]
    for d in order:
        there = got.at[behind(d)]
        copy(there, there, d, on_line(behind(d))).wait_recv()
        total = total + got[behind(d)]
    o_ref[chunk(me)] = total
    mine = o_ref.at[chunk(me)]
    outward = [copy(mine, mine, CHIPS - 1 + d, on_line(ahead(d))) for d in order]
    for one in outward:
        one.start()
    for d in order:
        there = o_ref.at[chunk(behind(d))]
        copy(there, there, CHIPS - 1 + d, on_line(behind(d))).wait_recv()
    for one in [first] + inward + outward:
        one.wait_send()


def joint_kernel(subs, g_ref, x_ref, gram_ref, o_ref, acc, from_left, from_right, swap, gs, gr, ssem, rsem):
    row = lax.axis_index("row")
    col = lax.axis_index("col")
    me, _, partner, left, right = line_places(row, col)
    greet(gather_peers(row, col) + [partner], [(me > 0, left), (me < CHIPS - 1, right)])
    gather = gather_steps(True, g_ref, gram_ref, gs, gr)
    reduce = reduce_steps(subs, x_ref, o_ref, acc, from_left, from_right, swap, ssem, rsem)
    for turn in "grrrgrgrrgrrrgrrrg":
        next(gather if turn == "g" else reduce, None)
    for rest in (reduce, gather):
        for _ in rest:
            pass


def cost(us):
    return pl.CostEstimate(flops=int(us * 1e9), bytes_accessed=int(us * 3e6), transcendentals=0)


def params(collective_id):
    return pltpu.CompilerParams(collective_id=collective_id, has_side_effects=True)


def dma(*shape):
    return pltpu.SemaphoreType.DMA(shape)


def gather_rows(block, collective_id):
    copies = gather_copies(False)
    return pl.pallas_call(
        rows_kernel,
        out_shape=jax.ShapeDtypeStruct((NY, NZH, NX) + block.shape, block.dtype),
        in_specs=[VMEM],
        out_specs=VMEM,
        scratch_shapes=[dma(copies), dma(copies)],
        compiler_params=params(collective_id),
        cost_estimate=cost(35),
        name="gather_rows",
    )(block)


def short_sum(halves, collective_id):
    _, rows, lanes = halves.shape
    half = pltpu.VMEM((rows, lanes), halves.dtype)
    return pl.pallas_call(
        short_sum_kernel,
        out_shape=jax.ShapeDtypeStruct((rows, lanes), halves.dtype),
        in_specs=[VMEM],
        out_specs=VMEM,
        scratch_shapes=[
            half,
            half,
            pltpu.VMEM((CHIPS, rows, lanes // CHIPS), halves.dtype),
            dma(2 * CHIPS - 1),
            dma(2 * CHIPS - 1),
        ],
        compiler_params=params(collective_id),
        cost_estimate=cost(20),
        name="short_sum",
    )(halves)


def joint(gram_half, halves, subs, collective_id):
    _, rows, lanes = halves.shape
    half = pltpu.VMEM((rows, lanes), halves.dtype)
    copies = gather_copies(True)
    return pl.pallas_call(
        functools.partial(joint_kernel, subs),
        out_shape=(
            jax.ShapeDtypeStruct((NY, NZH, NX, 2) + gram_half.shape, gram_half.dtype),
            jax.ShapeDtypeStruct(halves.shape, halves.dtype),
        ),
        in_specs=[VMEM, VMEM],
        out_specs=(VMEM, VMEM),
        scratch_shapes=[half] * 4 + [dma(copies), dma(copies), dma(6, CHIPS, subs), dma(6, CHIPS, subs)],
        compiler_params=params(collective_id),
        cost_estimate=cost(55),
        name="gram_and_sum",
    )(gram_half, halves)


def scaled_inverses(diag_blocks):
    order = diag_blocks.shape[-1]
    at_row = lax.broadcasted_iota(jnp.int32, (order, order), 0)
    at_col = lax.broadcasted_iota(jnp.int32, (order, order), 1)
    halves = 0.5 * jnp.sum(jnp.where(at_row == at_col, diag_blocks, 0.0), axis=2)
    strict = jnp.where(at_row < at_col, -diag_blocks / halves[:, :, None], 0.0)
    size = 16
    power = jnp.where(at_row // size == at_col // size, strict, 0.0)
    inverse = jnp.where(at_row == at_col, 1.0, power)
    for _ in range(3):
        power = matmul(power, power)
        inverse = inverse + matmul(inverse, power)
    while size < order:
        corner = jnp.where(
            jnp.logical_and(at_row // (2 * size) == at_col // (2 * size), at_row // size != at_col // size), strict, 0.0
        )
        inverse = inverse + matmul(matmul(inverse, corner), inverse)
        size *= 2
    return inverse, 1.0 / halves


def solve_turned(gram, product):
    order = gram.shape[0] // PANELS
    cut = lambda p: slice(p * order, (p + 1) * order)
    inverse, scale = scaled_inverses(jnp.stack([gram[cut(p), cut(p)] for p in range(PANELS)]))
    done = None
    for p in reversed(range(PANELS)):
        rest = product[:, cut(p)]
        if done is not None:
            rest = rest - contract(done, gram[cut(p), (p + 1) * order :], 1, 1)
        here = contract(rest * scale[p][None, :], inverse[p], 1, 1)
        done = here if done is None else jnp.concatenate([here, done], axis=1)
    return done


def permute_blocks(spread, owner_list, slot_list):
    blocks = owner_list.shape[0]
    target = owner_list * BLK_DEV + slot_list
    positions = jnp.arange(blocks, dtype=jnp.int32)
    one_hot = (target[:, None] == positions[None, :]).astype(jnp.float32)
    ordered = jnp.einsum(
        "rbw,bc->rcw",
        spread.reshape(spread.shape[0], blocks, BW),
        one_hot,
        precision=lax.Precision.HIGHEST,
        preferred_element_type=jnp.float32,
    )
    return ordered.reshape(spread.shape[0], blocks * BW)


def on_device(vectors, reflectors, owner_list, slot_list):
    panels, rows, width = reflectors.shape
    order = panels * width
    col = lax.axis_index("col")
    spread = lax.all_to_all(vectors, "col", split_axis=0, concat_axis=1, tiled=True)
    own_rows = jnp.transpose(reflectors, (1, 0, 2)).reshape(rows, order)
    panel_rows = gather_rows(own_rows, 0).reshape(NY * NZH * NX * rows, order)
    ordered = permute_blocks(spread, owner_list, slot_list)
    panel_rows, ordered = lax.optimization_barrier((panel_rows, ordered))
    slab_now = lax.all_to_all(ordered, "col", split_axis=1, concat_axis=0, tiled=True)
    share = order // (NY * NZH * NX)
    own_columns = lax.dynamic_slice_in_dim(panel_rows, col * share, share, axis=1)
    gram_part = contract(own_columns, panel_rows, 0, 0, lax.Precision.HIGHEST)
    gram_half = short_sum(gram_part.reshape(2, share // 2, order), 1)
    product_part = contract(slab_now, panel_rows, 0, 0)
    columns = product_part.shape[0]
    gram, product = joint(gram_half, product_part.reshape(2, columns // 2, order), 2, 2)
    turned = solve_turned(gram.reshape(order, order), product.reshape(columns, order))
    return slab_now - contract(panel_rows, turned, 1, 1)


def solution(mesh):
    return jax.shard_map(
        on_device,
        mesh=mesh,
        in_specs=(P("row", "col"), P(None, ("row", "col"), None), P(), P()),
        out_specs=P("row", "col"),
        check_vma=False,
    )
```

time: 328 us -> 217 us (0.66); the launches traced: 323 us -> 217 us
  Pallas kernels: 208 us -> 148 us
  matrix products: 46.6 us -> 23.8 us
  waiting for transfers between devices: 15.1 us -> 0.01 us
  starting transfers between devices: 45 us -> 38.5 us
  local copies, waits for them, and re-layouts: 6.75 us -> 3.34 us
    pallas_call x4 -> x3, Pallas kernels: 208 us -> 148 us  [the longest x1 69.2 us: joint(): pl.pallas_call(functools.partial(joint_kernel, subs), out_shape=(jax.Shap...]
    dot_general x22 -> x15, matrix products: 33.8 us -> 11.6 us  [the longest x14 11.2 us: matmul(): jnp.matmul(left, right, precision=lax.Precision.HIGH, preferred_element_t...]
    all_to_all x2, waiting for transfers between devices: 15.1 us -> 0.01 us  [the longest x1 0.01 us: on_device(): lax.all_to_all(ordered, 'col', split_axis=1, concat_axis=0, tiled=True)]
    all_to_all x2, starting transfers between devices: 45 us -> 38.5 us  [the longest x1 28 us: on_device(): lax.all_to_all(vectors, 'col', split_axis=0, concat_axis=1, tiled=True)]
    dot_general x3 -> x10, matrix products: 12.8 us -> 12.3 us  [contract(): lax.dot_general(left, right, (((left_dim,), (right_dim,)), ((), ())), pre...]
  transfers between devices with their start and end apart: 2 -> 2, of which waited for: 1 -> 0; matrix products, arithmetic and copies ran while one was open for 13% -> 2% of each run, Pallas kernels for 47% -> 37%
where the time goes in v2:
time: 217 us
  Pallas kernels  148 us (68%)
  starting transfers between devices  38.5 us (18%)
  matrix products  23.8 us (11%)
  local copies, waits for them, and re-layouts  3.34 us (2%)
  other arithmetic  2.29 us (1%)
    pallas_call x1, Pallas kernels, joint(): pl.pallas_call(functools.partial(joint_kernel, subs), out_shape=(jax.Shap...  69.2 us
    pallas_call x1, Pallas kernels, gather_rows(): pl.pallas_call(rows_kernel, out_shape=jax.ShapeDtypeStruct((NY, NZH, NX)...  47.5 us
    pallas_call x1, Pallas kernels, short_sum(): pl.pallas_call(short_sum_kernel, out_shape=jax.ShapeDtypeStruct((rows, la...  31.5 us
    all_to_all x1, starting transfers between devices, on_device(): lax.all_to_all(vectors, 'col', split_axis=0, concat_axis=1, tiled=True)  28 us
    dot_general x10, matrix products, contract(): lax.dot_general(left, right, (((left_dim,), (right_dim,)), ((), ())), pre...  12.3 us
    dot_general x14, matrix products, matmul(): jnp.matmul(left, right, precision=lax.Precision.HIGH, preferred_element_t...  11.2 us
    all_to_all x1, starting transfers between devices, on_device(): lax.all_to_all(ordered, 'col', split_axis=1, concat_axis=0, tiled=True)  10.5 us
  transfers between devices with their start and end apart: 2, of which 0 were waited for; matrix products, arithmetic and copies ran while one was open for 2% of the time, Pallas kernels for 37%

profile of v2, /device:TPU:1, one launch (start us, length us, event | category | flops | bytes accessed | tf_op | source)
XLA Modules:
  0.0 216.5 jit_solution(11216054478509994805)
XLA Ops:
  0.0 28.0 %all-to-all-start = ((f32[64,8,256]{2,1,0:T(8,128)}), f32[64,8,256]{2,1,0:T(8,128)S(1)}, u32[]{:S(2)}, u32[]{:S(2)}) async-start(f32[64,8,256]{2,1,0:T(8,128)} %bitcast.97), calls=%async_computation | async-start | bytes 1048576 | tf_op jit(solution)/shard_map/all_to_all | solution.py:527
  28.9 1.3 fusion.54
  30.1 47.5 %gather_rows.1 = f32[8,2,4,8,1024]{4,3,2,1,0:T(8,128)} custom-call(f32[8,1024]{1,0:T(8,128)} %bitcast.102), custom_call_target="tpu_custom_call" | custom-call | flops 35000000512 | bytes 105000000 | tf_op jit(solution)/shard_map/gather_rows/pallas_call | solution.py:421
  78.3 1.1 copy.11
  79.4 10.5 %all-to-all-start.1 = ((f32[8,64,256]{2,0,1:T(8,128)}), f32[8,64,256]{2,0,1:T(8,128)S(1)}, u32[]{:S(2)}, u32[]{:S(2)}) async-start(f32[8,64,256]{2,0,1:T(8,128)} %bitcast.7), calls=%async_computation.1 | async-start | bytes 1048576 | tf_op jit(solution)/shard_map/all_to_all | solution.py:532
  89.9 1.9 convolution_bitcast_fusion.1.x_ref
  91.7 31.5 %short_sum.1.g_ref = f32[8,1024]{1,0:T(8,128)} custom-call(f32[2,8,1024]{2,1,0:T(8,128)} %convolution_bitcast_fusion.1.x_ref), custom_call_target="tpu_custom_call" | custom-call | flops 20000000000 | bytes 60000000 | tf_op jit(solution)/shard_map/short_sum/pallas_call | solution.py:436
  123.5 2.1 fusion.x_ref
  125.6 69.2 %gram_and_sum.1 = (f32[8,2,4,2,8,1024]{5,4,3,2,1,0:T(8,128)}, f32[2,128,1024]{2,1,0:T(8,128)}) custom-call(f32[8,1024]{1,0:T(8,128)} %short_sum.1.g_ref, f32[2,128,1024]{2,1,0:T(8,128)} %fusion.x_ref), custom_call_target="tpu_custom_call" | custom-call | flops 54999998464 | bytes 165000000 | tf_op jit(solution)/shard_map/gram_and_sum/pallas_call | solution.py:458
  194.8 1.3 slice_bitcast_fusion.11
  196.3 1.1 fusion.21
  197.5 1.0 convolution_add_fusion.6
  199.9 0.7 convolution_add_fusion.5
  200.6 0.7 convolution_add_fusion.4
  201.3 0.9 fusion.18
  202.2 0.7 convolution_add_fusion.3
  202.8 0.9 fusion.16
  204.4 0.9 fusion.14
  206.0 0.9 fusion.12
  206.9 0.7 convolution_add_fusion
  208.5 1.6 fusion.3
  210.4 1.7 fusion.4
  212.4 1.9 fusion.2
  214.7 1.8 convolution_subtract_fusion
  (33 shorter events, 6.4 us)
Async XLA Ops:
  0.0 77.7 %all-to-all-start = ((f32[64,8,256]{2,1,0:T(8,128)}), f32[64,8,256]{2,1,0:T(8,128)S(1)}, u32[]{:S(2)}, u32[]{:S(2)}) async-start(f32[64,8,256]{2,1,0:T(8,128)} %bitcast.97), calls=%async_computation | async-start | bytes 1048576 | tf_op jit(solution)/shard_map/all_to_all | solution.py:527
  77.9 12.0 %copy-start = (f32[8,2,4,8,1024]{4,3,2,1,0:T(8,128)S(1)}, f32[8,2,4,8,1024]{4,3,2,1,0:T(8,128)}, u32[]{:S(2)}) copy-start(f32[8,2,4,8,1024]{4,3,2,1,0:T(8,128)} %gather_rows.1) | copy-start | bytes 6291460
  79.4 43.9 %all-to-all-start.1 = ((f32[8,64,256]{2,0,1:T(8,128)}), f32[8,64,256]{2,0,1:T(8,128)S(1)}, u32[]{:S(2)}, u32[]{:S(2)}) async-start(f32[8,64,256]{2,0,1:T(8,128)} %bitcast.7), calls=%async_computation.1 | async-start | bytes 1048576 | tf_op jit(solution)/shard_map/all_to_all | solution.py:532
  194.8 1.6 copy-start.2
  206.9 1.2 copy-start.1

commit v3 on v2

--- a/solution.py
+++ b/solution.py
@@ -336,10 +336,69 @@
     lax.fori_loop(0, CHIPS, finish, 0)
 
 
-def rows_kernel(x_ref, o_ref, ssem, rsem):
-    greet(gather_peers(lax.axis_index("row"), lax.axis_index("col")), [])
-    for _ in gather_steps(False, x_ref, o_ref, ssem, rsem):
+def resort_kernel(origin_ref, v_ref, x_ref, o_ref, s_ref, landed, ready, gs, gr, first_send, first_recv, last_send, last_recv):
+    row = lax.axis_index("row")
+    col = lax.axis_index("col")
+    cols = NY * NZH * NX
+    ahead = lambda d: lax.rem(col + d, cols)
+    behind = lambda d: lax.rem(col + cols - d, cols)
+    tiles = lambda c: pl.ds(BLK_DEV * c, BLK_DEV)
+    barrier = pltpu.get_barrier_semaphore()
+
+    def hello(d, _):
+        pl.semaphore_signal(barrier, inc=1, device_id=(row, ahead(d)), device_id_type=MESH)
+        return 0
+
+    lax.fori_loop(1, cols, hello, 0)
+    pl.semaphore_wait(barrier, cols - 1)
+
+    def deal(source, target, d, to, send_sem, recv_sem):
+        return pltpu.make_async_remote_copy(
+            src_ref=source,
+            dst_ref=target,
+            send_sem=send_sem.at[d],
+            recv_sem=recv_sem.at[d],
+            device_id=(row, to),
+            device_id_type=MESH,
+        )
+
+    def out(source, target, sems):
+        return lambda d: deal(source.at[tiles(ahead(d))], target.at[tiles(col)], d, ahead(d), *sems)
+
+    def coming(target, sems):
+        return lambda d: deal(target.at[tiles(behind(d))], target.at[tiles(behind(d))], d, behind(d), *sems)
+
+    first_sems, last_sems = (first_send, first_recv), (last_send, last_recv)
+    first_out, first_in = out(v_ref, landed, first_sems), coming(landed, first_sems)
+    last_out, last_in = out(ready, s_ref, last_sems), coming(s_ref, last_sems)
+
+    def each(act):
+        def body(d, _):
+            act(d)
+            return 0
+
+        lax.fori_loop(1, cols, body, 0)
+
+    gather = gather_steps(False, x_ref, o_ref, gs, gr)
+    next(gather)
+    each(lambda d: first_out(d).start())
+    landed[tiles(col)] = v_ref[tiles(col)]
+    for _ in range(3):
+        next(gather)
+    each(lambda d: first_in(d).wait_recv())
+
+    def move(t, _):
+        ready[t] = landed[origin_ref[t]]
+        return 0
+
+    lax.fori_loop(0, BLK_DEV * cols, move, 0)
+    each(lambda d: last_out(d).start())
+    s_ref[tiles(col)] = ready[tiles(col)]
+    for _ in gather:
         pass
+    each(lambda d: last_in(d).wait_recv())
+    each(lambda d: first_out(d).wait_send())
+    each(lambda d: last_out(d).wait_send())
 
 
 def short_sum_kernel(x_ref, o_ref, acc, swap, got, ssem, rsem):
@@ -416,18 +475,29 @@
     return pltpu.SemaphoreType.DMA(shape)
 
 
-def gather_rows(block, collective_id):
+def resort_and_gather(origin, vectors, block, collective_id):
     copies = gather_copies(False)
-    return pl.pallas_call(
-        rows_kernel,
-        out_shape=jax.ShapeDtypeStruct((NY, NZH, NX) + block.shape, block.dtype),
-        in_specs=[VMEM],
-        out_specs=VMEM,
-        scratch_shapes=[dma(copies), dma(copies)],
+    cols = NY * NZH * NX
+    tile = (8, BW)
+    height, width = vectors.shape
+    dealt = (height // tile[0], width // BW) + tile
+    flat = (dealt[0] * dealt[1],) + tile
+    tiled = jnp.transpose(vectors.reshape(dealt[0], tile[0], dealt[1], BW), (0, 2, 1, 3)).reshape(flat)
+    rows, slab = pl.pallas_call(
+        resort_kernel,
+        out_shape=(
+            jax.ShapeDtypeStruct((NY, NZH, NX) + block.shape, block.dtype),
+            jax.ShapeDtypeStruct(flat, vectors.dtype),
+        ),
+        in_specs=[pl.BlockSpec(memory_space=pltpu.SMEM), VMEM, VMEM],
+        out_specs=(VMEM, VMEM),
+        scratch_shapes=[pltpu.VMEM(flat, vectors.dtype)] * 2 + [dma(copies)] * 2 + [dma(cols)] * 4,
         compiler_params=params(collective_id),
-        cost_estimate=cost(35),
-        name="gather_rows",
-    )(block)
+        cost_estimate=cost(60),
+        name="resort_and_gather",
+    )(origin, tiled, block)
+    slab = jnp.transpose(slab.reshape(dealt), (0, 2, 1, 3)).reshape(height, width)
+    return rows.reshape(cols * block.shape[0], block.shape[1]), slab
 
 
 def short_sum(halves, collective_id):
@@ -505,31 +575,18 @@
     return done
 
 
-def permute_blocks(spread, owner_list, slot_list):
-    blocks = owner_list.shape[0]
+def origins(owner_list, slot_list):
     target = owner_list * BLK_DEV + slot_list
-    positions = jnp.arange(blocks, dtype=jnp.int32)
-    one_hot = (target[:, None] == positions[None, :]).astype(jnp.float32)
-    ordered = jnp.einsum(
-        "rbw,bc->rcw",
-        spread.reshape(spread.shape[0], blocks, BW),
-        one_hot,
-        precision=lax.Precision.HIGHEST,
-        preferred_element_type=jnp.float32,
-    )
-    return ordered.reshape(spread.shape[0], blocks * BW)
+    positions = jnp.arange(target.shape[0], dtype=jnp.int32)
+    return jnp.sum(jnp.where(positions[:, None] == target[None, :], positions[None, :], 0), axis=1)
 
 
 def on_device(vectors, reflectors, owner_list, slot_list):
     panels, rows, width = reflectors.shape
     order = panels * width
     col = lax.axis_index("col")
-    spread = lax.all_to_all(vectors, "col", split_axis=0, concat_axis=1, tiled=True)
     own_rows = jnp.transpose(reflectors, (1, 0, 2)).reshape(rows, order)
-    panel_rows = gather_rows(own_rows, 0).reshape(NY * NZH * NX * rows, order)
-    ordered = permute_blocks(spread, owner_list, slot_list)
-    panel_rows, ordered = lax.optimization_barrier((panel_rows, ordered))
-    slab_now = lax.all_to_all(ordered, "col", split_axis=1, concat_axis=0, tiled=True)
+    panel_rows, slab_now = resort_and_gather(origins(owner_list, slot_list), vectors, own_rows, 0)
     share = order // (NY * NZH * NX)
     own_columns = lax.dynamic_slice_in_dim(panel_rows, col * share, share, axis=1)
     gram_part = contract(own_columns, panel_rows, 0, 0, lax.Precision.HIGHEST)

time: 217 us -> 218 us (level)
  starting transfers between devices: 38.5 us -> 0 us
  Pallas kernels: 148 us -> 185 us
    all_to_all x2 -> x0, starting transfers between devices: 38.5 us -> none  [the longest x1 28 us: on_device(): lax.all_to_all(vectors, 'col', split_axis=0, concat_axis=1, tiled=True)]
    pallas_call x1, Pallas kernels: 47.5 us -> 80 us  [resort_and_gather(): pl.pallas_call(resort_kernel, out_shape=(jax.ShapeDtypeStruct((NY, NZH, N...]
    pallas_call x1, Pallas kernels: 31.5 us -> 41.7 us  [short_sum(): pl.pallas_call(short_sum_kernel, out_shape=jax.ShapeDtypeStruct((rows, la...]
    pallas_call x1, Pallas kernels: 69.2 us -> 63.2 us  [joint(): pl.pallas_call(functools.partial(joint_kernel, subs), out_shape=(jax.Shap...]
  transfers between devices with their start and end apart: 2 -> 0, of which waited for: 0 -> 0; matrix products, arithmetic and copies ran while one was open for 2% -> 0% of each run, Pallas kernels for 37% -> 0%
where the time goes in v3:
time: 218 us; the launch traced here: 217 us
  Pallas kernels  185 us (85%)
  matrix products  24.9 us (11%)
  local copies, waits for them, and re-layouts  3.74 us (2%)
  other arithmetic  3.08 us (1%)
    pallas_call x1, Pallas kernels, resort_and_gather(): pl.pallas_call(resort_kernel, out_shape=(jax.ShapeDtypeStruct((NY, NZH, N...  80 us
    pallas_call x1, Pallas kernels, joint(): pl.pallas_call(functools.partial(joint_kernel, subs), out_shape=(jax.Shap...  63.2 us
    pallas_call x1, Pallas kernels, short_sum(): pl.pallas_call(short_sum_kernel, out_shape=jax.ShapeDtypeStruct((rows, la...  41.7 us
    dot_general x10, matrix products, contract(): lax.dot_general(left, right, (((left_dim,), (right_dim,)), ((), ())), pre...  13.7 us
    dot_general x14, matrix products, matmul(): jnp.matmul(left, right, precision=lax.Precision.HIGH, preferred_element_t...  11.1 us

profile of v3, /device:TPU:1, one launch (start us, length us, event | category | flops | bytes accessed | tf_op | source)
XLA Modules:
  0.0 216.8 jit_solution(2399028507212137716)
XLA Ops:
  0.7 0.7 select_reduce_fusion.1.origin_ref
  1.5 1.4 fusion.51
  2.9 80.0 %resort_and_gather.1 = (f32[8,2,4,8,1024]{4,3,2,1,0:T(8,128)}, f32[128,8,128]{2,1,0:T(8,128)}) custom-call(s32[128]{0:T(128)} %select_reduce_fusion.1.origin_ref, f32[128,8,128]{2,1,0:T(8,128)} %bitcast.98, f32[8,1024]{1,0:T(8,128)} %bitcast.99), custom_call_target="tpu_custom_call" | custom-call | flops 60000002048 | bytes 180000000 | tf_op jit(solution)/shard_map/resort_and_gather/pallas_call | solution.py:486
  82.8 1.1 dynamic-slice_bitcast_fusion
  84.0 3.3 %fusion.56.x_ref = f32[2,8,1024]{2,1,0:T(8,128)} fusion(f32[512,1024,1]{1,0,2:T(8,128)} %bitcast.80, f32[16,512]{1,0:T(8,128)S(1)} %copy.7), kind=kOutput, calls=%fused_computation.93 | convolution fusion | flops 100663296 | bytes 2195456 | tf_op jit(solution)/shard_map/dot_general | solution.py:20
  87.4 41.7 %short_sum.1.g_ref = f32[8,1024]{1,0:T(8,128)} custom-call(f32[2,8,1024]{2,1,0:T(8,128)} %fusion.56.x_ref), custom_call_target="tpu_custom_call" | custom-call | flops 20000000000 | bytes 60000000 | tf_op jit(solution)/shard_map/short_sum/pallas_call | solution.py:506
  129.2 2.1 fusion.70.x_ref
  131.3 63.2 %gram_and_sum.1 = (f32[8,2,4,2,8,1024]{5,4,3,2,1,0:T(8,128)}, f32[2,128,1024]{2,1,0:T(8,128)}) custom-call(f32[8,1024]{1,0:T(8,128)} %short_sum.1.g_ref, f32[2,128,1024]{2,1,0:T(8,128)} %fusion.70.x_ref), custom_call_target="tpu_custom_call" | custom-call | flops 54999998464 | bytes 165000000 | tf_op jit(solution)/shard_map/gram_and_sum/pallas_call | solution.py:528
  194.6 1.3 slice_bitcast_fusion.11
  196.1 1.1 fusion.19
  197.2 1.0 convolution_add_fusion.6
  198.9 0.7 convolution_add_fusion.5
  200.3 0.7 convolution_add_fusion.4
  201.2 0.9 fusion.16
  202.1 0.7 convolution_add_fusion.3
  202.9 0.9 fusion.14
  203.8 0.7 convolution_add_fusion.2
  204.6 0.9 fusion.12
  205.5 0.7 convolution_add_fusion.1
  206.4 0.9 fusion.10
  209.0 1.3 fusion.1
  210.7 1.7 fusion.2
  212.7 1.9 fusion
  215.0 1.8 convolution_subtract_fusion
  (36 shorter events, 6.0 us)
Async XLA Ops:
  87.3 41.7 %copy-start.1 = (f32[128,8,128]{2,1,0:T(8,128)S(1)}, f32[128,8,128]{2,1,0:T(8,128)}, u32[]{:S(2)}) copy-start(f32[128,8,128]{2,1,0:T(8,128)} %get-tuple-element.9) | copy-start | bytes 1572868
  87.4 41.9 %copy-start = (f32[8,2,4,8,1024]{4,3,2,1,0:T(8,128)S(1)}, f32[8,2,4,8,1024]{4,3,2,1,0:T(8,128)}, u32[]{:S(2)}) copy-start(f32[8,2,4,8,1024]{4,3,2,1,0:T(8,128)} %get-tuple-element.10) | copy-start | bytes 6291460
  200.3 0.8 copy-start.6
  202.1 0.8 copy-start.5
  203.8 0.8 copy-start.4
  205.5 0.8 copy-start.3
  207.3 1.2 copy-start.2

commit v4 on v2

--- a/solution.py
+++ b/solution.py
@@ -176,10 +176,19 @@
 def reduce_steps(subs, x_ref, o_ref, acc, from_left, from_right, swap, ssem, rsem):
     me, core, partner, left, right = line_places(lax.axis_index("row"), lax.axis_index("col"))
     has_left, has_right = me > 0, me < CHIPS - 1
-    piece = acc.shape[0] // CHIPS // subs
+    rows, lanes = acc.shape[0] // CHIPS, acc.shape[1] * 2 // subs
+    across = subs // 2
 
     def part(j, q):
-        return (pl.ds(pl.multiple_of((j * subs + q) * piece, 8), piece), slice(None))
+        start = pl.multiple_of(j * rows + q // across * (rows // 2), 8)
+        return (pl.ds(start, rows // 2), pl.ds(pl.multiple_of(lax.rem(q, across) * lanes, BW), lanes))
+
+    def each_piece(act):
+        def body(q, _):
+            act(q)
+            return 0
+
+        lax.fori_loop(0, subs, body, 0)
 
     def copy(source, target, kind, j, q, to):
         return pltpu.make_async_remote_copy(
@@ -220,53 +229,55 @@
     for k in range(CHIPS // 2):
         order += [CHIPS - 1 - k, k]
     for j in order:
-        for q in range(subs):
-            swap_copy(j, q).start()
-    yield
+        each_piece(lambda q: swap_copy(j, q).start())
+    yield
+
+    def join(j, q):
+        swap_copy(j, q).wait_recv()
+        at = part(j, q)
+        acc[at] = x_ref[(core,) + at] + swap[at]
+
     for j in order:
-        for q in range(subs):
-            swap_copy(j, q).wait_recv()
+        each_piece(lambda q: join(j, q))
+
+    def inward(s, q):
+        @pl.when(jnp.logical_and(me <= s, has_right))
+        def _():
+            j = me + CHIPS - 1 - s
             at = part(j, q)
-            acc[at] = x_ref[(core,) + at] + swap[at]
+
+            @pl.when(has_left)
+            def _():
+                rightward(j, q).wait_recv()
+                from_left[at] = from_left[at] + acc[at]
+
+            @pl.when(jnp.logical_not(has_left))
+            def _():
+                from_left[at] = acc[at]
+
+            rightward(j, q).start()
+
+        @pl.when(jnp.logical_and(me >= CHIPS - 1 - s, has_left))
+        def _():
+            j = me - (CHIPS - 1) + s
+            at = part(j, q)
+
+            @pl.when(has_right)
+            def _():
+                leftward(j, q).wait_recv()
+                from_right[at] = from_right[at] + acc[at]
+
+            @pl.when(jnp.logical_not(has_right))
+            def _():
+                from_right[at] = acc[at]
+
+            leftward(j, q).start()
 
     for s in range(CHIPS - 1):
-        for q in range(subs):
-
-            @pl.when(jnp.logical_and(me <= s, has_right))
-            def _():
-                j = me + CHIPS - 1 - s
-                at = part(j, q)
-
-                @pl.when(has_left)
-                def _():
-                    rightward(j, q).wait_recv()
-                    from_left[at] = from_left[at] + acc[at]
-
-                @pl.when(jnp.logical_not(has_left))
-                def _():
-                    from_left[at] = acc[at]
-
-                rightward(j, q).start()
-
-            @pl.when(jnp.logical_and(me >= CHIPS - 1 - s, has_left))
-            def _():
-                j = me - (CHIPS - 1) + s
-                at = part(j, q)
-
-                @pl.when(has_right)
-                def _():
-                    leftward(j, q).wait_recv()
-                    from_right[at] = from_right[at] + acc[at]
-
-                @pl.when(jnp.logical_not(has_right))
-                def _():
-                    from_right[at] = acc[at]
-
-                leftward(j, q).start()
-
+        each_piece(lambda q: inward(s, q))
         yield
 
-    for q in range(subs):
+    def settle(q):
         at = part(me, q)
 
         @pl.when(has_left)
@@ -281,32 +292,44 @@
 
         o_ref[(core,) + at] = acc[at]
 
-    for s in range(CHIPS):
-        for q in range(subs):
-
-            @pl.when(me >= s)
-            def _():
-                j = me - s
-                if s:
-                    out_right(j, q).wait_recv()
-
-                @pl.when(has_right)
-                def _():
-                    out_right(j, q).start()
-
-                out_pair(j, q).start()
-
-            @pl.when(me <= CHIPS - 1 - s)
-            def _():
-                j = me + s
-                if s:
-                    out_left(j, q).wait_recv()
-                    out_pair(j, q).start()
-
-                @pl.when(has_left)
-                def _():
-                    out_left(j, q).start()
-
+        @pl.when(has_right)
+        def _():
+            out_right(me, q).start()
+
+        out_pair(me, q).start()
+
+        @pl.when(has_left)
+        def _():
+            out_left(me, q).start()
+
+    each_piece(settle)
+    yield
+
+    def outward(s, q):
+        @pl.when(me >= s)
+        def _():
+            j = me - s
+            out_right(j, q).wait_recv()
+
+            @pl.when(has_right)
+            def _():
+                out_right(j, q).start()
+
+            out_pair(j, q).start()
+
+        @pl.when(me <= CHIPS - 1 - s)
+        def _():
+            j = me + s
+            out_left(j, q).wait_recv()
+
+            @pl.when(has_left)
+            def _():
+                out_left(j, q).start()
+
+            out_pair(j, q).start()
+
+    for s in range(1, CHIPS):
+        each_piece(lambda q: outward(s, q))
         yield
 
     def finish(j, _):
@@ -336,13 +359,64 @@
     lax.fori_loop(0, CHIPS, finish, 0)
 
 
-def rows_kernel(x_ref, o_ref, ssem, rsem):
-    greet(gather_peers(lax.axis_index("row"), lax.axis_index("col")), [])
-    for _ in gather_steps(False, x_ref, o_ref, ssem, rsem):
+def exchange(row, col, send_sem, recv_sem, source, target, started):
+    cols = NY * NZH * NX
+    tiles = lambda c: pl.ds(BLK_DEV * c, BLK_DEV)
+
+    def copy(d):
+        other = lax.rem(col + d, cols) if started else lax.rem(col + cols - d, cols)
+        here = target.at[tiles(col if started else other)]
+        return pltpu.make_async_remote_copy(
+            src_ref=source.at[tiles(other)] if started else here,
+            dst_ref=here,
+            send_sem=send_sem.at[d],
+            recv_sem=recv_sem.at[d],
+            device_id=(row, other),
+            device_id_type=MESH,
+        )
+
+    def each(act):
+        def body(d, _):
+            act(copy(d))
+            return 0
+
+        lax.fori_loop(1, cols, body, 0)
+
+    return each
+
+
+def greet_col(row, col, others):
+    cols = NY * NZH * NX
+    barrier = pltpu.get_barrier_semaphore()
+
+    def hello(d, _):
+        pl.semaphore_signal(barrier, inc=1, device_id=(row, lax.rem(col + d, cols)), device_id_type=MESH)
+        return 0
+
+    lax.fori_loop(1, cols, hello, 0)
+    for other in others:
+        pl.semaphore_signal(barrier, inc=1, device_id=other, device_id_type=MESH)
+    pl.semaphore_wait(barrier, cols - 1 + len(others))
+
+
+def deal_kernel(v_ref, x_ref, o_ref, landed, gs, gr, send_sem, recv_sem):
+    row = lax.axis_index("row")
+    col = lax.axis_index("col")
+    own = pl.ds(BLK_DEV * col, BLK_DEV)
+    greet_col(row, col, [])
+    out = exchange(row, col, send_sem, recv_sem, v_ref, landed, True)
+    coming = exchange(row, col, send_sem, recv_sem, v_ref, landed, False)
+    gather = gather_steps(False, x_ref, o_ref, gs, gr)
+    next(gather)
+    out(lambda one: one.start())
+    landed[own] = v_ref[own]
+    for _ in gather:
         pass
-
-
-def short_sum_kernel(x_ref, o_ref, acc, swap, got, ssem, rsem):
+    coming(lambda one: one.wait_recv())
+    out(lambda one: one.wait_send())
+
+
+def short_sum_steps(x_ref, o_ref, acc, swap, got, ssem, rsem):
     row = lax.axis_index("row")
     col = lax.axis_index("col")
     core = lax.rem(row, 2)
@@ -354,7 +428,6 @@
     lanes = acc.shape[1] // CHIPS
     chunk = lambda j: (slice(None), pl.ds(pl.multiple_of(j * lanes, lanes), lanes))
     order = list(range(1, CHIPS))
-    greet([partner] + [on_line(ahead(d)) for d in order], [])
 
     def copy(source, target, number, to):
         return pltpu.make_async_remote_copy(
@@ -373,6 +446,7 @@
     inward = [copy(acc.at[chunk(ahead(d))], got.at[me], d, on_line(ahead(d))) for d in order]
     for one in inward:
         one.start()
+    yield
     total = acc[chunk(me)]
     for d in order:
         there = got.at[behind(d)]
@@ -383,11 +457,36 @@
     outward = [copy(mine, mine, CHIPS - 1 + d, on_line(ahead(d))) for d in order]
     for one in outward:
         one.start()
+    yield
     for d in order:
         there = o_ref.at[chunk(behind(d))]
         copy(there, there, CHIPS - 1 + d, on_line(behind(d))).wait_recv()
     for one in [first] + inward + outward:
         one.wait_send()
+
+
+def return_kernel(origin_ref, landed, x_ref, s_ref, o_ref, ready, acc, swap, got, ssem, rsem, send_sem, recv_sem):
+    row = lax.axis_index("row")
+    col = lax.axis_index("col")
+    me, core, partner, _, _ = line_places(row, col)
+    own = pl.ds(BLK_DEV * col, BLK_DEV)
+    greet_col(row, col, [partner] + [(2 * lax.rem(me + d, CHIPS) + core, col) for d in range(1, CHIPS)])
+    short = short_sum_steps(x_ref, o_ref, acc, swap, got, ssem, rsem)
+    next(short)
+
+    def move(t, _):
+        ready[t] = landed[origin_ref[t]]
+        return 0
+
+    lax.fori_loop(0, ready.shape[0], move, 0)
+    out = exchange(row, col, send_sem, recv_sem, ready, s_ref, True)
+    coming = exchange(row, col, send_sem, recv_sem, ready, s_ref, False)
+    out(lambda one: one.start())
+    s_ref[own] = ready[own]
+    for _ in short:
+        pass
+    coming(lambda one: one.wait_recv())
+    out(lambda one: one.wait_send())
 
 
 def joint_kernel(subs, g_ref, x_ref, gram_ref, o_ref, acc, from_left, from_right, swap, gs, gr, ssem, rsem):
@@ -416,39 +515,62 @@
     return pltpu.SemaphoreType.DMA(shape)
 
 
-def gather_rows(block, collective_id):
+def tiles_of(slab):
+    height, width = slab.shape
+    tiled = slab.reshape(height // 8, 8, width // BW, BW)
+    return jnp.transpose(tiled, (0, 2, 1, 3)).reshape(-1, 8, BW)
+
+
+def from_tiles(tiles, height, width):
+    tiled = tiles.reshape(height // 8, width // BW, 8, BW)
+    return jnp.transpose(tiled, (0, 2, 1, 3)).reshape(height, width)
+
+
+def deal_and_gather(tiles, block, collective_id):
     copies = gather_copies(False)
-    return pl.pallas_call(
-        rows_kernel,
-        out_shape=jax.ShapeDtypeStruct((NY, NZH, NX) + block.shape, block.dtype),
-        in_specs=[VMEM],
-        out_specs=VMEM,
-        scratch_shapes=[dma(copies), dma(copies)],
+    cols = NY * NZH * NX
+    rows, landed = pl.pallas_call(
+        deal_kernel,
+        out_shape=(
+            jax.ShapeDtypeStruct((NY, NZH, NX) + block.shape, block.dtype),
+            jax.ShapeDtypeStruct(tiles.shape, tiles.dtype),
+        ),
+        in_specs=[VMEM, VMEM],
+        out_specs=(VMEM, VMEM),
+        scratch_shapes=[dma(copies)] * 2 + [dma(cols)] * 2,
         compiler_params=params(collective_id),
-        cost_estimate=cost(35),
-        name="gather_rows",
-    )(block)
-
-
-def short_sum(halves, collective_id):
+        cost_estimate=cost(40),
+        name="deal_and_gather",
+    )(tiles, block)
+    return rows.reshape(cols * block.shape[0], block.shape[1]), landed
+
+
+def return_and_sum(origin, landed, halves, collective_id):
     _, rows, lanes = halves.shape
     half = pltpu.VMEM((rows, lanes), halves.dtype)
+    cols = NY * NZH * NX
     return pl.pallas_call(
-        short_sum_kernel,
-        out_shape=jax.ShapeDtypeStruct((rows, lanes), halves.dtype),
-        in_specs=[VMEM],
-        out_specs=VMEM,
+        return_kernel,
+        out_shape=(
+            jax.ShapeDtypeStruct(landed.shape, landed.dtype),
+            jax.ShapeDtypeStruct((rows, lanes), halves.dtype),
+        ),
+        in_specs=[pl.BlockSpec(memory_space=pltpu.SMEM), VMEM, VMEM],
+        out_specs=(VMEM, VMEM),
         scratch_shapes=[
+            pltpu.VMEM(landed.shape, landed.dtype),
             half,
             half,
             pltpu.VMEM((CHIPS, rows, lanes // CHIPS), halves.dtype),
             dma(2 * CHIPS - 1),
             dma(2 * CHIPS - 1),
+            dma(cols),
+            dma(cols),
         ],
         compiler_params=params(collective_id),
-        cost_estimate=cost(20),
-        name="short_sum",
-    )(halves)
+        cost_estimate=cost(35),
+        name="return_and_sum",
+    )(origin, landed, halves)
 
 
 def joint(gram_half, halves, subs, collective_id):
@@ -505,38 +627,27 @@
     return done
 
 
-def permute_blocks(spread, owner_list, slot_list):
-    blocks = owner_list.shape[0]
+def origins(owner_list, slot_list):
     target = owner_list * BLK_DEV + slot_list
-    positions = jnp.arange(blocks, dtype=jnp.int32)
-    one_hot = (target[:, None] == positions[None, :]).astype(jnp.float32)
-    ordered = jnp.einsum(
-        "rbw,bc->rcw",
-        spread.reshape(spread.shape[0], blocks, BW),
-        one_hot,
-        precision=lax.Precision.HIGHEST,
-        preferred_element_type=jnp.float32,
-    )
-    return ordered.reshape(spread.shape[0], blocks * BW)
+    positions = jnp.arange(target.shape[0], dtype=jnp.int32)
+    return jnp.sum(jnp.where(positions[:, None] == target[None, :], positions[None, :], 0), axis=1)
 
 
 def on_device(vectors, reflectors, owner_list, slot_list):
     panels, rows, width = reflectors.shape
     order = panels * width
     col = lax.axis_index("col")
-    spread = lax.all_to_all(vectors, "col", split_axis=0, concat_axis=1, tiled=True)
     own_rows = jnp.transpose(reflectors, (1, 0, 2)).reshape(rows, order)
-    panel_rows = gather_rows(own_rows, 0).reshape(NY * NZH * NX * rows, order)
-    ordered = permute_blocks(spread, owner_list, slot_list)
-    panel_rows, ordered = lax.optimization_barrier((panel_rows, ordered))
-    slab_now = lax.all_to_all(ordered, "col", split_axis=1, concat_axis=0, tiled=True)
+    panel_rows, landed = deal_and_gather(tiles_of(vectors), own_rows, 0)
     share = order // (NY * NZH * NX)
     own_columns = lax.dynamic_slice_in_dim(panel_rows, col * share, share, axis=1)
     gram_part = contract(own_columns, panel_rows, 0, 0, lax.Precision.HIGHEST)
-    gram_half = short_sum(gram_part.reshape(2, share // 2, order), 1)
+    origin = origins(owner_list, slot_list)
+    tiles, gram_half = return_and_sum(origin, landed, gram_part.reshape(2, share // 2, order), 1)
+    slab_now = from_tiles(tiles, *vectors.shape)
     product_part = contract(slab_now, panel_rows, 0, 0)
     columns = product_part.shape[0]
-    gram, product = joint(gram_half, product_part.reshape(2, columns // 2, order), 2, 2)
+    gram, product = joint(gram_half, product_part.reshape(2, columns // 2, order), 4, 2)
     turned = solve_turned(gram.reshape(order, order), product.reshape(columns, order))
     return slab_now - contract(panel_rows, turned, 1, 1)
 

time: 217 us -> 225 us (1.037)
  Pallas kernels: 148 us -> 192 us
  starting transfers between devices: 38.5 us -> 0 us
    pallas_call x2, Pallas kernels: 79 us -> 124 us  [the longest x1 69.5 us: deal_and_gather(): pl.pallas_call(deal_kernel, out_shape=(jax.ShapeDtypeStruct((NY, NZH, NX)...]
    all_to_all x2 -> x0, starting transfers between devices: 38.5 us -> none  [the longest x1 28 us: on_device(): lax.all_to_all(vectors, 'col', split_axis=0, concat_axis=1, tiled=True)]
  transfers between devices with their start and end apart: 2 -> 0, of which waited for: 0 -> 0; matrix products, arithmetic and copies ran while one was open for 2% -> 0% of each run, Pallas kernels for 37% -> 0%
where the time goes in v4:
time: 225 us; the launch traced here: 224 us
  Pallas kernels  192 us (85%)
  matrix products  24.9 us (11%)
  local copies, waits for them, and re-layouts  4.28 us (2%)
  other arithmetic  3 us (1%)
    pallas_call x1, Pallas kernels, deal_and_gather(): pl.pallas_call(deal_kernel, out_shape=(jax.ShapeDtypeStruct((NY, NZH, NX)...  69.5 us
    pallas_call x1, Pallas kernels, joint(): pl.pallas_call(functools.partial(joint_kernel, subs), out_shape=(jax.Shap...  68 us
    pallas_call x1, Pallas kernels, return_and_sum(): pl.pallas_call(return_kernel, out_shape=(jax.ShapeDtypeStruct(landed.shap...  54.5 us
    dot_general x10, matrix products, contract(): lax.dot_general(left, right, (((left_dim,), (right_dim,)), ((), ())), pre...  13.5 us
    dot_general x14, matrix products, matmul(): jnp.matmul(left, right, precision=lax.Precision.HIGH, preferred_element_t...  11.4 us

profile of v4, /device:TPU:1, one launch (start us, length us, event | category | flops | bytes accessed | tf_op | source)
XLA Modules:
  0.0 224.5 jit_solution(6670969803545716322)
XLA Ops:
  1.4 1.4 fusion.51
  2.8 69.5 %deal_and_gather.1 = (f32[8,2,4,8,1024]{4,3,2,1,0:T(8,128)}, f32[128,8,128]{2,1,0:T(8,128)}) custom-call(f32[128,8,128]{2,1,0:T(8,128)} %bitcast.98, f32[8,1024]{1,0:T(8,128)} %bitcast.99), custom_call_target="tpu_custom_call" | custom-call | flops 40000000000 | bytes 120000000 | tf_op jit(solution)/shard_map/deal_and_gather/pallas_call | solution.py:532
  72.3 1.1 dynamic-slice_bitcast_fusion
  73.5 3.3 %fusion.56.x_ref = f32[2,8,1024]{2,1,0:T(8,128)} fusion(f32[512,1024,1]{1,0,2:T(8,128)} %bitcast.80, f32[16,512]{1,0:T(8,128)S(1)} %copy.7), kind=kOutput, calls=%fused_computation.93 | convolution fusion | flops 100663296 | bytes 2195456 | tf_op jit(solution)/shard_map/dot_general | solution.py:20
  76.8 54.5 %return_and_sum.1 = (f32[128,8,128]{2,1,0:T(8,128)}, f32[8,1024]{1,0:T(8,128)}) custom-call(s32[128]{0:T(128)} %select_reduce_fusion.1.origin_ref, f32[128,8,128]{2,1,0:T(8,128)} %get-tuple-element.11.landed, f32[2,8,1024]{2,1,0:T(8,128)} %fusion.56.x_ref), custom_call_target="tpu_custom_call" | custom-call | flops 35000000512 | bytes 105000000 | tf_op jit(solution)/shard_map/return_and_sum/pallas_call | solution.py:552
  131.3 1.2 copy.9
  132.6 2.1 fusion.70.x_ref
  134.7 68.0 %gram_and_sum.1 = (f32[8,2,4,2,8,1024]{5,4,3,2,1,0:T(8,128)}, f32[2,128,1024]{2,1,0:T(8,128)}) custom-call(f32[8,1024]{1,0:T(8,128)} %get-tuple-element.14.g_ref, f32[2,128,1024]{2,1,0:T(8,128)} %fusion.70.x_ref), custom_call_target="tpu_custom_call" | custom-call | flops 54999998464 | bytes 165000000 | tf_op jit(solution)/shard_map/gram_and_sum/pallas_call | solution.py:580
  202.7 1.3 slice_bitcast_fusion.11
  204.2 1.1 fusion.19
  205.3 1.0 convolution_add_fusion.6
  207.0 0.7 convolution_add_fusion.5
  208.4 0.7 convolution_add_fusion.4
  209.1 0.9 fusion.16
  210.7 0.9 fusion.14
  211.6 0.7 convolution_add_fusion.2
  212.4 0.9 fusion.12
  213.3 0.7 convolution_add_fusion.1
  214.2 0.9 fusion.10
  215.1 0.9 convolution_add_fusion
  216.6 1.3 fusion.1
  218.3 1.7 fusion.2
  220.3 1.9 fusion
  222.6 1.8 convolution_subtract_fusion
  (32 shorter events, 5.7 us)
Async XLA Ops:
  76.8 55.7 %copy-start = (f32[8,2,4,8,1024]{4,3,2,1,0:T(8,128)S(1)}, f32[8,2,4,8,1024]{4,3,2,1,0:T(8,128)}, u32[]{:S(2)}) copy-start(f32[8,2,4,8,1024]{4,3,2,1,0:T(8,128)} %get-tuple-element.12) | copy-start | bytes 6291460
  211.6 0.8 copy-start.4
  213.3 0.8 copy-start.3
  215.1 1.2 copy-start.2
  220.0 2.6 %copy-start.1 = (f32[128,8,128]{2,1,0:T(8,128)S(1)}, f32[128,8,128]{2,1,0:T(8,128)}, u32[]{:S(2)}) copy-start(f32[128,8,128]{2,1,0:T(8,128)} %get-tuple-element.13) | copy-start | bytes 1572868

commit v5 on v2

--- a/solution.py
+++ b/solution.py
@@ -168,15 +168,20 @@
 
 def line_places(row, col):
     core = lax.rem(row, 2)
-    right = (jnp.minimum(row + 2, 2 * CHIPS - 2 + core), col)
-    left = (jnp.maximum(row - 2, core), col)
-    return row // 2, core, (row + 1 - 2 * core, col), left, right
-
-
-def reduce_steps(subs, x_ref, o_ref, acc, from_left, from_right, swap, ssem, rsem):
-    me, core, partner, left, right = line_places(lax.axis_index("row"), lax.axis_index("col"))
-    has_left, has_right = me > 0, me < CHIPS - 1
+    chip = row // 2
+    parity = lax.rem(chip, 2)
+    right = (jnp.minimum(row + 4, 2 * CHIPS - 4 + 2 * parity + core), col)
+    left = (jnp.maximum(row - 4, 2 * parity + core), col)
+    return chip // 2, parity, core, (row + 1 - 2 * core, col), (row + 2 - 4 * parity, col), left, right
+
+
+def reduce_steps(subs, x_ref, o_ref, acc, near, from_left, from_right, swap, ssem, rsem):
+    me, parity, core, partner, mate, left, right = line_places(lax.axis_index("row"), lax.axis_index("col"))
+    length = CHIPS // 2
+    has_left, has_right = me > 0, me < length - 1
     piece = acc.shape[0] // CHIPS // subs
+    mine = lambda b: 2 * b + parity
+    others = lambda b: 2 * b + 1 - parity
 
     def part(j, q):
         return (pl.ds(pl.multiple_of((j * subs + q) * piece, 8), piece), slice(None))
@@ -191,149 +196,199 @@
             device_id_type=MESH,
         )
 
+    def here(buffer, kind, to):
+        return lambda j, q: copy(buffer.at[part(j, q)], buffer.at[part(j, q)], kind, j, q, to)
+
     def swap_copy(j, q):
         return copy(x_ref.at[(1 - core,) + part(j, q)], swap.at[part(j, q)], 0, j, q, partner)
 
-    def rightward(j, q):
-        return copy(from_left.at[part(j, q)], from_left.at[part(j, q)], 1, j, q, right)
-
-    def leftward(j, q):
-        return copy(from_right.at[part(j, q)], from_right.at[part(j, q)], 2, j, q, left)
-
-    def o_at(j, q):
-        return o_ref.at[(core,) + part(j, q)]
-
-    def out_right(j, q):
-        return copy(o_at(j, q), o_at(j, q), 3, j, q, right)
-
-    def out_left(j, q):
-        return copy(o_at(j, q), o_at(j, q), 4, j, q, left)
-
-    def out_pair(j, q):
-        return copy(o_at(j, q), o_at(j, q), 5, j, q, partner)
+    def to_mate(j, q):
+        return copy(acc.at[part(j, q)], near.at[part(j, q)], 1, j, q, mate)
+
+    rightward, leftward = here(from_left, 2, right), here(from_right, 3, left)
+
+    def out(kind, to):
+        def made(j, q):
+            place = o_ref.at[(core,) + part(j, q)]
+            return copy(place, place, kind, j, q, to)
+
+        return made
+
+    out_right, out_left, out_mate, out_pair = out(4, right), out(5, left), out(6, mate), out(7, partner)
 
     def other_pair(j, q):
         there = o_ref.at[(1 - core,) + part(j, q)]
-        return copy(there, there, 5, j, q, partner)
+        return copy(there, there, 7, j, q, partner)
+
+    def joined(j, q):
+        swap_copy(j, q).wait_recv()
+        at = part(j, q)
+        return x_ref[(core,) + at] + swap[at]
+
+    def with_mate(j, q):
+        value = joined(j, q)
+        to_mate(j, q).wait_recv()
+        return value + near[part(j, q)]
 
     order = []
-    for k in range(CHIPS // 2):
-        order += [CHIPS - 1 - k, k]
-    for j in order:
+    for k in range(length // 2):
+        order += [length - 1 - k, k]
+    for b in order:
         for q in range(subs):
-            swap_copy(j, q).start()
-    yield
-    for j in order:
+            swap_copy(others(b), q).start()
+            swap_copy(mine(b), q).start()
+    yield
+    for b in order:
         for q in range(subs):
-            swap_copy(j, q).wait_recv()
-            at = part(j, q)
-            acc[at] = x_ref[(core,) + at] + swap[at]
-
-    for s in range(CHIPS - 1):
+            acc[part(others(b), q)] = joined(others(b), q)
+            to_mate(others(b), q).start()
+    yield
+
+    for s in range(length - 1):
         for q in range(subs):
 
             @pl.when(jnp.logical_and(me <= s, has_right))
             def _():
-                j = me + CHIPS - 1 - s
+                j = mine(me + length - 1 - s)
                 at = part(j, q)
+                value = with_mate(j, q)
 
                 @pl.when(has_left)
                 def _():
                     rightward(j, q).wait_recv()
-                    from_left[at] = from_left[at] + acc[at]
+                    from_left[at] = from_left[at] + value
 
                 @pl.when(jnp.logical_not(has_left))
                 def _():
-                    from_left[at] = acc[at]
+                    from_left[at] = value
 
                 rightward(j, q).start()
 
-            @pl.when(jnp.logical_and(me >= CHIPS - 1 - s, has_left))
+            @pl.when(jnp.logical_and(me >= length - 1 - s, has_left))
             def _():
-                j = me - (CHIPS - 1) + s
+                j = mine(me - (length - 1) + s)
                 at = part(j, q)
+                value = with_mate(j, q)
 
                 @pl.when(has_right)
                 def _():
                     leftward(j, q).wait_recv()
-                    from_right[at] = from_right[at] + acc[at]
+                    from_right[at] = from_right[at] + value
 
                 @pl.when(jnp.logical_not(has_right))
                 def _():
-                    from_right[at] = acc[at]
+                    from_right[at] = value
 
                 leftward(j, q).start()
 
         yield
 
     for q in range(subs):
-        at = part(me, q)
+        j = mine(me)
+        at = part(j, q)
+        acc[at] = with_mate(j, q)
 
         @pl.when(has_left)
         def _():
-            rightward(me, q).wait_recv()
+            rightward(j, q).wait_recv()
             acc[at] = acc[at] + from_left[at]
 
         @pl.when(has_right)
         def _():
-            leftward(me, q).wait_recv()
+            leftward(j, q).wait_recv()
             acc[at] = acc[at] + from_right[at]
 
         o_ref[(core,) + at] = acc[at]
 
-    for s in range(CHIPS):
+        @pl.when(has_right)
+        def _():
+            out_right(j, q).start()
+
+        @pl.when(has_left)
+        def _():
+            out_left(j, q).start()
+
+        out_mate(j, q).start()
+        out_pair(j, q).start()
+
+    yield
+
+    def pass_on(b, q):
+        out_mate(others(b), q).wait_recv()
+        out_pair(others(b), q).start()
+
+    for s in range(1, length + 1):
         for q in range(subs):
-
-            @pl.when(me >= s)
-            def _():
-                j = me - s
-                if s:
+            if s < length:
+
+                @pl.when(me >= s)
+                def _():
+                    j = mine(me - s)
                     out_right(j, q).wait_recv()
 
-                @pl.when(has_right)
-                def _():
-                    out_right(j, q).start()
-
-                out_pair(j, q).start()
-
-            @pl.when(me <= CHIPS - 1 - s)
-            def _():
-                j = me + s
-                if s:
+                    @pl.when(has_right)
+                    def _():
+                        out_right(j, q).start()
+
+                    out_mate(j, q).start()
+                    out_pair(j, q).start()
+
+                @pl.when(me <= length - 1 - s)
+                def _():
+                    j = mine(me + s)
                     out_left(j, q).wait_recv()
+
+                    @pl.when(has_left)
+                    def _():
+                        out_left(j, q).start()
+
+                    out_mate(j, q).start()
                     out_pair(j, q).start()
 
-                @pl.when(has_left)
-                def _():
-                    out_left(j, q).start()
+            if s == 1:
+                pass_on(me, q)
+            else:
+
+                @pl.when(me >= s - 1)
+                def _():
+                    pass_on(me - (s - 1), q)
+
+                @pl.when(me <= length - s)
+                def _():
+                    pass_on(me + (s - 1), q)
 
         yield
 
-    def finish(j, _):
+    def finish(b, _):
         for q in range(subs):
+            j = mine(b)
             swap_copy(j, q).wait_send()
-
-            @pl.when(jnp.logical_and(has_right, j > me))
+            swap_copy(others(b), q).wait_send()
+            to_mate(others(b), q).wait_send()
+
+            @pl.when(jnp.logical_and(has_right, b > me))
             def _():
                 rightward(j, q).wait_send()
 
-            @pl.when(jnp.logical_and(has_left, j < me))
+            @pl.when(jnp.logical_and(has_left, b < me))
             def _():
                 leftward(j, q).wait_send()
 
-            @pl.when(jnp.logical_and(has_right, j <= me))
+            @pl.when(jnp.logical_and(has_right, b <= me))
             def _():
                 out_right(j, q).wait_send()
 
-            @pl.when(jnp.logical_and(has_left, j >= me))
+            @pl.when(jnp.logical_and(has_left, b >= me))
             def _():
                 out_left(j, q).wait_send()
 
-            out_pair(j, q).wait_send()
-            other_pair(j, q).wait_recv()
+            out_mate(j, q).wait_send()
+            for k in (j, others(b)):
+                out_pair(k, q).wait_send()
+                other_pair(k, q).wait_recv()
         return 0
 
-    lax.fori_loop(0, CHIPS, finish, 0)
+    lax.fori_loop(0, length, finish, 0)
 
 
 def rows_kernel(x_ref, o_ref, ssem, rsem):
@@ -390,14 +445,14 @@
         one.wait_send()
 
 
-def joint_kernel(subs, g_ref, x_ref, gram_ref, o_ref, acc, from_left, from_right, swap, gs, gr, ssem, rsem):
+def joint_kernel(subs, g_ref, x_ref, gram_ref, o_ref, acc, near, from_left, from_right, swap, gs, gr, ssem, rsem):
     row = lax.axis_index("row")
     col = lax.axis_index("col")
-    me, _, partner, left, right = line_places(row, col)
-    greet(gather_peers(row, col) + [partner], [(me > 0, left), (me < CHIPS - 1, right)])
+    me, _, _, partner, mate, left, right = line_places(row, col)
+    greet(gather_peers(row, col) + [partner, mate], [(me > 0, left), (me < CHIPS // 2 - 1, right)])
     gather = gather_steps(True, g_ref, gram_ref, gs, gr)
-    reduce = reduce_steps(subs, x_ref, o_ref, acc, from_left, from_right, swap, ssem, rsem)
-    for turn in "grrrgrgrrgrrrgrrrg":
+    reduce = reduce_steps(subs, x_ref, o_ref, acc, near, from_left, from_right, swap, ssem, rsem)
+    for turn in "grrgrrgrgrrgrrg":
         next(gather if turn == "g" else reduce, None)
     for rest in (reduce, gather):
         for _ in rest:
@@ -463,7 +518,7 @@
         ),
         in_specs=[VMEM, VMEM],
         out_specs=(VMEM, VMEM),
-        scratch_shapes=[half] * 4 + [dma(copies), dma(copies), dma(6, CHIPS, subs), dma(6, CHIPS, subs)],
+        scratch_shapes=[half] * 5 + [dma(copies), dma(copies), dma(8, CHIPS, subs), dma(8, CHIPS, subs)],
         compiler_params=params(collective_id),
         cost_estimate=cost(55),
         name="gram_and_sum",

time: 217 us -> 208 us (0.959)
  Pallas kernels: 148 us -> 139 us
    pallas_call x1, Pallas kernels: 69.2 us -> 60.4 us  [joint(): pl.pallas_call(functools.partial(joint_kernel, subs), out_shape=(jax.Shap...]
  transfers between devices with their start and end apart: 2 -> 2, of which waited for: 0 -> 0; matrix products, arithmetic and copies ran while one was open for 2% -> 2% of each run, Pallas kernels for 37% -> 38%
where the time goes in v5:
time: 208 us
  Pallas kernels  139 us (67%)
  starting transfers between devices  38.5 us (19%)
  matrix products  23.8 us (11%)
  local copies, waits for them, and re-layouts  3.34 us (2%)
  other arithmetic  2.29 us (1%)
    pallas_call x1, Pallas kernels, joint(): pl.pallas_call(functools.partial(joint_kernel, subs), out_shape=(jax.Shap...  60.4 us
    pallas_call x1, Pallas kernels, gather_rows(): pl.pallas_call(rows_kernel, out_shape=jax.ShapeDtypeStruct((NY, NZH, NX)...  47.5 us
    pallas_call x1, Pallas kernels, short_sum(): pl.pallas_call(short_sum_kernel, out_shape=jax.ShapeDtypeStruct((rows, la...  31.5 us
    all_to_all x1, starting transfers between devices, on_device(): lax.all_to_all(vectors, 'col', split_axis=0, concat_axis=1, tiled=True)  28 us
    dot_general x10, matrix products, contract(): lax.dot_general(left, right, (((left_dim,), (right_dim,)), ((), ())), pre...  12.3 us
    dot_general x14, matrix products, matmul(): jnp.matmul(left, right, precision=lax.Precision.HIGH, preferred_element_t...  11.2 us
    all_to_all x1, starting transfers between devices, on_device(): lax.all_to_all(ordered, 'col', split_axis=1, concat_axis=0, tiled=True)  10.5 us
  transfers between devices with their start and end apart: 2, of which 0 were waited for; matrix products, arithmetic and copies ran while one was open for 2% of the time, Pallas kernels for 38%

profile of v5, /device:TPU:1, one launch (start us, length us, event | category | flops | bytes accessed | tf_op | source)
XLA Modules:
  0.0 207.8 jit_solution(5744883767333610704)
XLA Ops:
  0.0 28.0 %all-to-all-start = ((f32[64,8,256]{2,1,0:T(8,128)}), f32[64,8,256]{2,1,0:T(8,128)S(1)}, u32[]{:S(2)}, u32[]{:S(2)}) async-start(f32[64,8,256]{2,1,0:T(8,128)} %bitcast.97), calls=%async_computation | async-start | bytes 1048576 | tf_op jit(solution)/shard_map/all_to_all | solution.py:582
  28.9 1.3 fusion.54
  30.1 47.5 %gather_rows.1 = f32[8,2,4,8,1024]{4,3,2,1,0:T(8,128)} custom-call(f32[8,1024]{1,0:T(8,128)} %bitcast.102), custom_call_target="tpu_custom_call" | custom-call | flops 35000000512 | bytes 105000000 | tf_op jit(solution)/shard_map/gather_rows/pallas_call | solution.py:476
  78.3 1.1 copy.11
  79.4 10.5 %all-to-all-start.1 = ((f32[8,64,256]{2,0,1:T(8,128)}), f32[8,64,256]{2,0,1:T(8,128)S(1)}, u32[]{:S(2)}, u32[]{:S(2)}) async-start(f32[8,64,256]{2,0,1:T(8,128)} %bitcast.7), calls=%async_computation.1 | async-start | bytes 1048576 | tf_op jit(solution)/shard_map/all_to_all | solution.py:587
  89.9 1.9 convolution_bitcast_fusion.1.x_ref
  91.7 31.5 %short_sum.1.g_ref = f32[8,1024]{1,0:T(8,128)} custom-call(f32[2,8,1024]{2,1,0:T(8,128)} %convolution_bitcast_fusion.1.x_ref), custom_call_target="tpu_custom_call" | custom-call | flops 20000000000 | bytes 60000000 | tf_op jit(solution)/shard_map/short_sum/pallas_call | solution.py:491
  123.5 2.1 %fusion.x_ref = f32[2,128,1024]{2,1,0:T(8,128)} fusion(f32[2,128,512]{2,1,0:T(8,128)S(1)} %bitcast.87, f32[512,1024]{1,0:T(8,128)S(1)} %bitcast.84), kind=kOutput, calls=%fused_computation | convolution fusion | flops 805306368 | bytes 3670016 | tf_op jit(solution)/shard_map/dot_general | solution.py:20
  125.6 60.4 %gram_and_sum.1 = (f32[8,2,4,2,8,1024]{5,4,3,2,1,0:T(8,128)}, f32[2,128,1024]{2,1,0:T(8,128)}) custom-call(f32[8,1024]{1,0:T(8,128)} %short_sum.1.g_ref, f32[2,128,1024]{2,1,0:T(8,128)} %fusion.x_ref), custom_call_target="tpu_custom_call" | custom-call | flops 54999998464 | bytes 165000000 | tf_op jit(solution)/shard_map/gram_and_sum/pallas_call | solution.py:513
  186.1 1.3 slice_bitcast_fusion.11
  187.6 1.1 fusion.21
  188.7 1.0 convolution_add_fusion.6
  191.8 0.7 convolution_add_fusion.4
  192.5 0.9 fusion.18
  193.4 0.7 convolution_add_fusion.3
  194.1 0.9 fusion.16
  195.7 0.9 fusion.14
  196.6 0.7 convolution_add_fusion.1
  197.3 0.9 fusion.12
  198.2 0.7 convolution_add_fusion
  200.0 1.3 fusion.3
  201.7 1.7 fusion.4
  203.7 1.9 fusion.2
  206.0 1.8 convolution_subtract_fusion
  (33 shorter events, 6.6 us)
Async XLA Ops:
  0.0 77.7 %all-to-all-start = ((f32[64,8,256]{2,1,0:T(8,128)}), f32[64,8,256]{2,1,0:T(8,128)S(1)}, u32[]{:S(2)}, u32[]{:S(2)}) async-start(f32[64,8,256]{2,1,0:T(8,128)} %bitcast.97), calls=%async_computation | async-start | bytes 1048576 | tf_op jit(solution)/shard_map/all_to_all | solution.py:582
  77.9 12.0 %copy-start = (f32[8,2,4,8,1024]{4,3,2,1,0:T(8,128)S(1)}, f32[8,2,4,8,1024]{4,3,2,1,0:T(8,128)}, u32[]{:S(2)}) copy-start(f32[8,2,4,8,1024]{4,3,2,1,0:T(8,128)} %gather_rows.1) | copy-start | bytes 6291460
  79.4 43.9 %all-to-all-start.1 = ((f32[8,64,256]{2,0,1:T(8,128)}), f32[8,64,256]{2,0,1:T(8,128)S(1)}, u32[]{:S(2)}, u32[]{:S(2)}) async-start(f32[8,64,256]{2,0,1:T(8,128)} %bitcast.7), calls=%async_computation.1 | async-start | bytes 1048576 | tf_op jit(solution)/shard_map/all_to_all | solution.py:587
  186.0 1.6 copy-start.2
  198.2 1.2 copy-start.1

commit v6 on v5

--- a/solution.py
+++ b/solution.py
@@ -71,8 +71,8 @@
     def device(yy, zz, xx):
         return (row, (yy * NZH + zz) * NX + xx)
 
-    def spot(yy, zz, xx, lanes):
-        middle = (core,) if pair else ()
+    def spot(yy, zz, xx, lanes, of=core):
+        middle = (of,) if pair else ()
         return o_ref.at[(yy, zz, xx) + middle + (everything, lanes)]
 
     def launch(source, target, to):
@@ -111,6 +111,14 @@
     def finish(waits):
         for target, number, origin in waits:
             arrived(target, number, origin)
+
+    def hand_over(swaps, region, p):
+        swaps.append((region(p, 1 - core), launch(region(p, core), region(p, core), partner), partner))
+
+    def finish_and_hand(swaps, waits, length, place, region):
+        for (target, number, origin), d in zip(waits, sorted(range(1, length), key=lambda d: -min(d, length - d))):
+            arrived(target, number, origin)
+            hand_over(swaps, region, lax.rem(place + length - d, length))
 
     def by_y(zz, xx, part, first):
         return spread(NY, y, lambda p: spot(p, zz, xx, lanes_of[part]), first, lambda p: device(p, zh, x))
@@ -137,33 +145,36 @@
     far_y = by_y(far, x, 1, None)
     far_x = by_x(far, y, 0, None)
     yield
+    swaps = []
+    far_columns = lambda p, of: spot(everything, far, p, lanes_of[1], of)
+    far_rows = lambda p, of: spot(p, far, everything, lanes_of[0], of)
     finish(far_y)
     far_wide_x = by_x(far, everything, 1, None)
     finish(far_x)
     far_wide_y = by_y(far, everything, 0, None)
+    if pair:
+        hand_over(swaps, far_columns, x)
+        hand_over(swaps, far_rows, y)
     yield
     finish(wide_x)
     finish(wide_y)
 
-    def half_of(zz, cc):
-        return o_ref.at[:, zz, :, cc]
-
     if pair:
-        first_swap = launch(half_of(zh, core), half_of(zh, core), partner)
-    yield
-    finish(far_wide_x)
-    finish(far_wide_y)
-    if pair:
-        second_swap = launch(half_of(far, core), half_of(far, core), partner)
+        hand_over(swaps, lambda p, of: o_ref.at[:, p, :, of], zh)
         yield
-        arrived(half_of(zh, 1 - core), first_swap, partner)
-        arrived(half_of(far, 1 - core), second_swap, partner)
+        finish_and_hand(swaps, far_wide_x, NX, x, far_columns)
+        finish_and_hand(swaps, far_wide_y, NY, y, far_rows)
+        yield
+        finish(swaps)
+    else:
+        finish(far_wide_x)
+        finish(far_wide_y)
     for copy in sent:
         copy.wait_send()
 
 
 def gather_copies(pair):
-    return 1 + 4 * (NX - 1 + NY - 1) + (2 if pair else 0)
+    return 1 + 4 * (NX - 1 + NY - 1) + (1 + NX + NY if pair else 0)
 
 
 def line_places(row, col):
@@ -452,7 +463,7 @@
     greet(gather_peers(row, col) + [partner, mate], [(me > 0, left), (me < CHIPS // 2 - 1, right)])
     gather = gather_steps(True, g_ref, gram_ref, gs, gr)
     reduce = reduce_steps(subs, x_ref, o_ref, acc, near, from_left, from_right, swap, ssem, rsem)
-    for turn in "grrgrrgrgrrgrrg":
+    for turn in "grrgrgrrgrrgrrg":
         next(gather if turn == "g" else reduce, None)
     for rest in (reduce, gather):
         for _ in rest:

time: 208 us -> 209 us (level)
  no operation moved by 1% of the time
where the time goes in v6:
time: 209 us; the launch traced here: 208 us
  Pallas kernels  140 us (67%)
  starting transfers between devices  38.5 us (18%)
  matrix products  23.8 us (11%)
  local copies, waits for them, and re-layouts  3.34 us (2%)
  other arithmetic  2.29 us (1%)
    pallas_call x1, Pallas kernels, joint(): pl.pallas_call(functools.partial(joint_kernel, subs), out_shape=(jax.Shap...  60.7 us
    pallas_call x1, Pallas kernels, gather_rows(): pl.pallas_call(rows_kernel, out_shape=jax.ShapeDtypeStruct((NY, NZH, NX)...  47.5 us
    pallas_call x1, Pallas kernels, short_sum(): pl.pallas_call(short_sum_kernel, out_shape=jax.ShapeDtypeStruct((rows, la...  31.5 us
    all_to_all x1, starting transfers between devices, on_device(): lax.all_to_all(vectors, 'col', split_axis=0, concat_axis=1, tiled=True)  28 us
    dot_general x10, matrix products, contract(): lax.dot_general(left, right, (((left_dim,), (right_dim,)), ((), ())), pre...  12.3 us
    dot_general x14, matrix products, matmul(): jnp.matmul(left, right, precision=lax.Precision.HIGH, preferred_element_t...  11.2 us
    all_to_all x1, starting transfers between devices, on_device(): lax.all_to_all(ordered, 'col', split_axis=1, concat_axis=0, tiled=True)  10.5 us
  transfers between devices with their start and end apart: 2, of which 0 were waited for; matrix products, arithmetic and copies ran while one was open for 2% of the time, Pallas kernels for 38%

profile of v6, /device:TPU:1, one launch (start us, length us, event | category | flops | bytes accessed | tf_op | source)
XLA Modules:
  0.0 208.1 jit_solution(9720722505884565926)
XLA Ops:
  0.0 28.0 %all-to-all-start = ((f32[64,8,256]{2,1,0:T(8,128)}), f32[64,8,256]{2,1,0:T(8,128)S(1)}, u32[]{:S(2)}, u32[]{:S(2)}) async-start(f32[64,8,256]{2,1,0:T(8,128)} %bitcast.97), calls=%async_computation | async-start | bytes 1048576 | tf_op jit(solution)/shard_map/all_to_all | solution.py:593
  28.9 1.3 fusion.54
  30.1 47.5 %gather_rows.1 = f32[8,2,4,8,1024]{4,3,2,1,0:T(8,128)} custom-call(f32[8,1024]{1,0:T(8,128)} %bitcast.102), custom_call_target="tpu_custom_call" | custom-call | flops 35000000512 | bytes 105000000 | tf_op jit(solution)/shard_map/gather_rows/pallas_call | solution.py:487
  78.3 1.1 copy.11
  79.4 10.5 %all-to-all-start.1 = ((f32[8,64,256]{2,0,1:T(8,128)}), f32[8,64,256]{2,0,1:T(8,128)S(1)}, u32[]{:S(2)}, u32[]{:S(2)}) async-start(f32[8,64,256]{2,0,1:T(8,128)} %bitcast.7), calls=%async_computation.1 | async-start | bytes 1048576 | tf_op jit(solution)/shard_map/all_to_all | solution.py:598
  89.9 1.9 convolution_bitcast_fusion.1.x_ref
  91.7 31.5 %short_sum.1.g_ref = f32[8,1024]{1,0:T(8,128)} custom-call(f32[2,8,1024]{2,1,0:T(8,128)} %convolution_bitcast_fusion.1.x_ref), custom_call_target="tpu_custom_call" | custom-call | flops 20000000000 | bytes 60000000 | tf_op jit(solution)/shard_map/short_sum/pallas_call | solution.py:502
  123.5 2.1 %fusion.x_ref = f32[2,128,1024]{2,1,0:T(8,128)} fusion(f32[2,128,512]{2,1,0:T(8,128)S(1)} %bitcast.87, f32[512,1024]{1,0:T(8,128)S(1)} %bitcast.84), kind=kOutput, calls=%fused_computation | convolution fusion | flops 805306368 | bytes 3670016 | tf_op jit(solution)/shard_map/dot_general | solution.py:20
  125.6 60.7 %gram_and_sum.1 = (f32[8,2,4,2,8,1024]{5,4,3,2,1,0:T(8,128)}, f32[2,128,1024]{2,1,0:T(8,128)}) custom-call(f32[8,1024]{1,0:T(8,128)} %short_sum.1.g_ref, f32[2,128,1024]{2,1,0:T(8,128)} %fusion.x_ref), custom_call_target="tpu_custom_call" | custom-call | flops 54999998464 | bytes 165000000 | tf_op jit(solution)/shard_map/gram_and_sum/pallas_call | solution.py:524
  186.3 1.3 slice_bitcast_fusion.11
  187.9 1.1 fusion.21
  189.0 1.0 convolution_add_fusion.6
  191.4 0.7 convolution_add_fusion.5
  192.1 0.7 convolution_add_fusion.4
  192.8 0.9 fusion.18
  193.7 0.7 convolution_add_fusion.3
  194.4 0.9 fusion.16
  196.0 0.9 fusion.14
  197.6 0.9 fusion.12
  198.5 0.7 convolution_add_fusion
  200.3 1.3 fusion.3
  202.0 1.7 fusion.4
  204.0 1.9 fusion.2
  206.3 1.8 convolution_subtract_fusion
  (33 shorter events, 6.6 us)
Async XLA Ops:
  0.0 77.7 %all-to-all-start = ((f32[64,8,256]{2,1,0:T(8,128)}), f32[64,8,256]{2,1,0:T(8,128)S(1)}, u32[]{:S(2)}, u32[]{:S(2)}) async-start(f32[64,8,256]{2,1,0:T(8,128)} %bitcast.97), calls=%async_computation | async-start | bytes 1048576 | tf_op jit(solution)/shard_map/all_to_all | solution.py:593
  77.9 12.0 %copy-start = (f32[8,2,4,8,1024]{4,3,2,1,0:T(8,128)S(1)}, f32[8,2,4,8,1024]{4,3,2,1,0:T(8,128)}, u32[]{:S(2)}) copy-start(f32[8,2,4,8,1024]{4,3,2,1,0:T(8,128)} %gather_rows.1) | copy-start | bytes 6291460
  79.4 43.9 %all-to-all-start.1 = ((f32[8,64,256]{2,0,1:T(8,128)}), f32[8,64,256]{2,0,1:T(8,128)S(1)}, u32[]{:S(2)}, u32[]{:S(2)}) async-start(f32[8,64,256]{2,0,1:T(8,128)} %bitcast.7), calls=%async_computation.1 | async-start | bytes 1048576 | tf_op jit(solution)/shard_map/all_to_all | solution.py:598
  186.3 1.6 copy-start.2
  198.5 1.2 copy-start.1
